TPU v7x, 128 devices: a whole 4x4x4 slice. The times are simulated.
128 devices in a mesh: dp: 4 (over y), dict: 32 (over x, z, core).
Axes of the slice: x: 4, y: 4, z: 4, core: 2. Of those that a mesh axis runs over, the one named last changes fastest.
Arguments:
- acts: bfloat16 [8192, 8192], P('dict', 'dp'), may hold values from -6 to 6
- lists: int32 [512, 2], P('dict'), may hold values from 0 to 31, all different within a row; in each aligned block of 16 rows (0 to 15, 16 to 31, ...) at most 2 rows name the same one
- w_enc: bfloat16 [8192, 32768], P('dp', 'dict'), may hold values from -0.0625 to 0.0625
- w_dec: bfloat16 [32768, 8192], P('dict', 'dp'), may hold values from -0.1875 to 0.1875
- b_enc: bfloat16 [32768], P('dict'), may hold values from -3 to 3
- b_dec: bfloat16 [8192], P('dp'), may hold values from -3 to 3
Outputs:
- grad_enc: bfloat16 [8192, 32768], P('dp', 'dict')
- grad_dec: bfloat16 [32768, 8192], P('dict', 'dp')
Inputs may be any that keep to these rules, and one draw needn't show every extreme that they name: Each row block lists 2 different panels. Among the 16 row blocks of one index of dict, no panel is listed by more than 2 blocks, and some panel is listed by exactly 2.
All inputs are finite; a program needn't handle non-finite values.
Results may differ from a plain program's by a relative error of at most 0.0057.
Values may be sent and summed in bfloat16 or wider, within the bound.
No kernel may reach another device: no remote copies, remote signals or barrier semaphores. Data moves between devices by JAX's collectives and lax.ppermute only.
A program may use at most 128 MiB of HBM per device.

v0:
```python
import jax
import jax.numpy as jnp
from jax import lax
from jax.sharding import PartitionSpec as P


def on_device(acts, lists, w_enc, w_dec, b_enc, b_dec):
    peers = lax.axis_size("dict")
    block_count = lists.shape[0]
    active_count = lists.shape[1]
    rows_block = acts.shape[0] // block_count
    feature_cols = acts.shape[1]
    capacity = max(2, (2 * block_count * active_count + peers - 1) // peers)
    slot_total = peers * capacity
    flat_ids = lists.reshape(-1)
    onehot = (flat_ids[:, None] == jnp.arange(peers, dtype=jnp.int32)[None, :]).astype(jnp.int32)
    rank_index = jnp.sum((jnp.cumsum(onehot, axis=0) - 1) * onehot, axis=1)
    slot_index = flat_ids * capacity + rank_index
    item_block = jnp.arange(block_count * active_count, dtype=jnp.int32) // active_count
    slot_match = (jnp.arange(slot_total, dtype=jnp.int32)[:, None] == slot_index[None, :]).astype(
        jnp.float32
    )
    block_match = (item_block[:, None] == jnp.arange(block_count, dtype=jnp.int32)[None, :]).astype(
        jnp.float32
    )
    selector = jnp.dot(slot_match, block_match).astype(jnp.bfloat16)
    block_rows = acts.reshape(block_count, rows_block * feature_cols)
    outgoing = jnp.dot(selector, block_rows, preferred_element_type=jnp.float32).astype(
        jnp.bfloat16
    )
    outgoing = outgoing.reshape(peers, capacity * rows_block, feature_cols)
    received = lax.all_to_all(outgoing, "dict", split_axis=0, concat_axis=0, tiled=True)
    rows_in = received.reshape(-1, feature_cols)
    pre_local = jnp.dot(rows_in, w_enc, preferred_element_type=jnp.float32)
    bias_enc = b_enc.astype(jnp.float32)
    preact = lax.psum(pre_local, "dp") + bias_enc
    activity = (jnp.maximum(preact, 0.0) ** 2).astype(jnp.bfloat16)
    part = jnp.dot(activity, w_dec, preferred_element_type=jnp.float32).astype(jnp.bfloat16)
    part = part.reshape(peers, capacity * rows_block, feature_cols)
    returned = lax.all_to_all(part, "dict", split_axis=0, concat_axis=0, tiled=True)
    returned = returned.reshape(slot_total, rows_block * feature_cols)
    rebuilt = lax.dot_general(
        selector, returned, (((0,), (0,)), ((), ())), preferred_element_type=jnp.float32
    )
    rebuilt = rebuilt.reshape(block_count * rows_block, feature_cols) + b_dec.astype(jnp.float32)
    residual_g = ((rebuilt - acts.astype(jnp.float32)) * (1.0 / rows_block)).astype(jnp.bfloat16)
    resid_out = jnp.dot(
        selector,
        residual_g.reshape(block_count, rows_block * feature_cols),
        preferred_element_type=jnp.float32,
    ).astype(jnp.bfloat16)
    resid_out = resid_out.reshape(peers, capacity * rows_block, feature_cols)
    residual_in = lax.all_to_all(
        resid_out, "dict", split_axis=0, concat_axis=0, tiled=True
    ).reshape(-1, feature_cols)
    grad_dec = lax.dot_general(
        activity, residual_in, (((0,), (0,)), ((), ())), preferred_element_type=jnp.float32
    ).astype(jnp.bfloat16)
    dact_local = lax.dot_general(
        residual_in, w_dec, (((1,), (1,)), ((), ())), preferred_element_type=jnp.float32
    )
    dact = lax.psum(dact_local, "dp")
    grad_pre = (dact * 2.0 * jnp.maximum(preact, 0.0)).astype(jnp.bfloat16)
    grad_enc = lax.dot_general(
        rows_in, grad_pre, (((0,), (0,)), ((), ())), preferred_element_type=jnp.float32
    ).astype(jnp.bfloat16)
    return (grad_enc, grad_dec)


def solution(mesh):
    in_specs = (
        P("dict", "dp"),
        P("dict", None),
        P("dp", "dict"),
        P("dict", "dp"),
        P("dict"),
        P("dp"),
    )
    out_specs = (P("dp", "dict"), P("dict", "dp"))
    return jax.shard_map(
        on_device, mesh=mesh, in_specs=in_specs, out_specs=out_specs, check_vma=False
    )
```

profile of v0, /device:TPU:1, one launch (start us, length us, event | category | flops | bytes accessed | tf_op | source)
XLA Modules:
  0.0 449.6 jit_solution(6548300190928002087)
XLA Ops:
  7.2 0.8 copy.9
  8.4 1.6 reshape.59
  10.2 3.3 convolution_convert_fusion.1
  13.5 7.4 %reshape.60 = bf16[32,32,2048]{2,1,0:T(8,128)(2,1)} reshape(bf16[64,32768]{1,0:T(8,128)(2,1)} %convolution_convert_fusion.1) | data formatting | bytes 8388608 | tf_op jit(solution)/shard_map/reshape | solution.py:31
  20.9 60.3 %all_to_all.15 = bf16[32,32,2048]{2,1,0:T(8,128)(2,1)S(1)} all-to-all(bf16[32,32,2048]{2,1,0:T(8,128)(2,1)} %reshape.60), channel_id=1, replica_groups=mesh['dp'=4,'dict'=32] {'dict'}, dimensions={0} | all-to-all | bytes 8388608 | tf_op jit(solution)/shard_map/all_to_all | solution.py:32
  81.2 2.0 copy-done
  83.1 6.0 %fusion.10 = f32[1024,1024]{1,0:T(8,128)} fusion(bf16[1024,2048]{1,0:T(8,128)(2,1)S(1)} %bitcast.16, bf16[2048,1024]{1,0:T(8,128)(2,1)S(1)} %copy-done.5), kind=kOutput, calls=%fused_computation.29 | convolution fusion | flops 4294967296 | bytes 12582912 | tf_op jit(solution)/shard_map/dot_general | solution.py:34
  89.8 89.8 %all-reduce.3.cloned.1.call-done = f32[1024,1024]{1,0:T(8,128)} async-done(((f32[1024,1024]{1,0:T(8,128)}), f32[1024,1024]{1,0:T(8,128)}) %all-reduce.3.cloned.1.call-update) | async-done | bytes 4194320 | tf_op jit(solution)/shard_map/psum | solution.py:36
  179.6 10.0 %convolution_convert_fusion.4 = bf16[1024,2048]{1,0:T(8,128)(2,1)} fusion(bf16[1024,2048]{1,0:T(8,128)(2,1)} %param.9, f32[1024,1024]{1,0:T(8,128)} %all-reduce.3.cloned.1.call-done, f32[1024]{0:T(1024)S(1)} %convert_element_type.44), kind=kOutput, calls=%fused_computation.7 | convolution fusion | flops 4301258752 | bytes 12587008 | tf_op jit(solution)/shard_map/dot_general | solution.py:38
  189.6 8.0 %all-to-all-start.1 = ((bf16[32,32,2048]{2,1,0:T(8,128)(2,1)}), bf16[32,32,2048]{2,1,0:T(8,128)(2,1)}, u32[]{:S(2)}, u32[]{:S(2)}) async-start(bf16[32,32,2048]{2,1,0:T(8,128)(2,1)} %bitcast.20), calls=%async_computation.1 | async-start | bytes 8388608 | tf_op jit(solution)/shard_map/all_to_all | solution.py:40
  197.7 52.0 %all-to-all-done.1 = bf16[32,32,2048]{2,1,0:T(8,128)(2,1)} async-done(((bf16[32,32,2048]{2,1,0:T(8,128)(2,1)}), bf16[32,32,2048]{2,1,0:T(8,128)(2,1)}, u32[]{:S(2)}, u32[]{:S(2)}) %all-to-all-start.1) | async-done | bytes 4194336 | tf_op jit(solution)/shard_map/all_to_all | solution.py:40
  249.7 7.4 %reshape.63 = bf16[64,32768]{1,0:T(8,128)(2,1)} reshape(bf16[32,32,2048]{2,1,0:T(8,128)(2,1)} %all-to-all-done.1) | data formatting | bytes 8388608 | tf_op jit(solution)/shard_map/reshape | solution.py:41
  257.1 4.3 fusion.11
  261.4 1.7 reshape.64
  263.1 1.3 multiply_convert_fusion.3
  264.5 1.6 reshape.65
  266.0 3.3 convolution_convert_fusion
  269.3 7.4 %reshape.66 = bf16[32,32,2048]{2,1,0:T(8,128)(2,1)} reshape(bf16[64,32768]{1,0:T(8,128)(2,1)} %convolution_convert_fusion) | data formatting | bytes 8388608 | tf_op jit(solution)/shard_map/reshape | solution.py:52
  276.7 57.9 %all_to_all.16 = bf16[32,32,2048]{2,1,0:T(8,128)(2,1)S(1)} all-to-all(bf16[32,32,2048]{2,1,0:T(8,128)(2,1)} %reshape.66), channel_id=1, replica_groups=mesh['dp'=4,'dict'=32] {'dict'}, dimensions={0} | all-to-all | bytes 8388608 | tf_op jit(solution)/shard_map/all_to_all | solution.py:53
  334.6 1.9 copy-done.1
  336.5 6.1 %fusion.12 = f32[1024,1024]{1,0:T(8,128)} fusion(bf16[1024,2048]{1,0:T(8,128)(2,1)S(1)} %bitcast.18, bf16[1024,2048]{1,0:T(8,128)(2,1)S(1)} %copy-done.6), kind=kOutput, calls=%fused_computation.31 | convolution fusion | flops 4294967296 | bytes 12582912 | tf_op jit(solution)/shard_map/dot_general | solution.py:59
  342.6 10.1 %convolution_convert_fusion.2 = bf16[1024,2048]{1,0:T(8,128)(2,1)} fusion(bf16[1024,2048]{1,0:T(8,128)(2,1)} %bitcast.19, f32[1024,1024]{1,0:T(8,128)} %all-reduce.3.cloned.1.call-done, f32[1024]{0:T(1024)S(1)} %convert_element_type.44), kind=kOutput, calls=%fused_computation.5 | convolution fusion | flops 4301258752 | bytes 12587008 | tf_op jit(solution)/shard_map/dot_general | solution.py:56
  352.7 78.8 %all-reduce.5.cloned.1.call-done = f32[1024,1024]{1,0:T(8,128)} async-done(((f32[1024,1024]{1,0:T(8,128)}), f32[1024,1024]{1,0:T(8,128)}) %all-reduce.5.cloned.1.call-update) | async-done | bytes 4194320 | tf_op jit(solution)/shard_map/psum | solution.py:62
  431.5 11.3 %convolution_convert_fusion.3 = bf16[2048,1024]{1,0:T(8,128)(2,1)} fusion(bf16[1024,2048]{1,0:T(8,128)(2,1)} %bitcast.17, f32[1024,1024]{1,0:T(8,128)} %all-reduce.5.cloned.1.call-done, f32[1024,1024]{1,0:T(8,128)} %all-reduce.3.cloned.1.call-done, f32[1024]{0:T(1024)S(1)} %convert_element_type.44), kind=kOutput, calls=%fused_computation.6 | convolution fusion | flops 4302307328 | bytes 16781312 | tf_op jit(solution)/shard_map/dot_general | solution.py:64
  (24 shorter events, 1.4 us)
Async XLA Ops:
  7.2 172.5 %all-reduce.3.cloned.1.call-start = ((), (), s32[]{:S(2)}) async-start(), calls=%async_computation.3 | async-start | bytes 8388608 | tf_op jit(solution)/shard_map/psum | solution.py:36
  20.9 62.3 %copy-start.5 = (bf16[2048,1024]{1,0:T(8,128)(2,1)S(1)}, bf16[2048,1024]{1,0:T(8,128)(2,1)}, u32[]{:S(2)}) copy-start(bf16[2048,1024]{1,0:T(8,128)(2,1)} %param.8) | copy-start | bytes 12582916
  81.2 2.0 copy-start
  89.1 0.7 copy-start.4
  189.6 8.1 %copy-start.3 = (bf16[2048]{0:T(1024)(128)(2,1)S(1)}, bf16[2048]{0:T(1024)(128)(2,1)}, u32[]{:S(2)}) copy-start(bf16[2048]{0:T(1024)(128)(2,1)} %param.11) | copy-start | bytes 12292
  189.6 60.1 %all-to-all-start.1 = ((bf16[32,32,2048]{2,1,0:T(8,128)(2,1)}), bf16[32,32,2048]{2,1,0:T(8,128)(2,1)}, u32[]{:S(2)}, u32[]{:S(2)}) async-start(bf16[32,32,2048]{2,1,0:T(8,128)(2,1)} %bitcast.20), calls=%async_computation.1 | async-start | bytes 8388608 | tf_op jit(solution)/shard_map/all_to_all | solution.py:40
  197.6 233.8 %all-reduce.5.cloned.1.call-start = ((), (), s32[]{:S(2)}) async-start(), calls=%async_computation.4 | async-start | bytes 8388608 | tf_op jit(solution)/shard_map/psum | solution.py:62
  257.1 6.0 %copy-start.2 = (bf16[256,2048]{1,0:T(8,128)(2,1)S(1)}, bf16[256,2048]{1,0:T(8,128)(2,1)}, u32[]{:S(2)}) copy-start(bf16[256,2048]{1,0:T(8,128)(2,1)} %param.6) | copy-start | bytes 3145732
  276.7 59.9 %copy-start.6 = (bf16[1024,2048]{1,0:T(8,128)(2,1)S(1)}, bf16[1024,2048]{1,0:T(8,128)(2,1)}, u32[]{:S(2)}) copy-start(bf16[1024,2048]{1,0:T(8,128)(2,1)} %param.9) | copy-start | bytes 12582916
  334.6 1.9 copy-start.1
Sparse Core Ops, SparseCore 0:
  89.3 90.3 all-reduce.2
  342.7 88.6 all-reduce.4
where the time goes:
time: 450 us
  waiting for transfers between devices  221 us (49%)
  blocking collectives  118 us (26%)
  matrix products  54.5 us (12%)
  local copies, waits for them, and re-layouts  32.4 us (7%)
  between operations  14.1 us (3%)
  starting transfers between devices  8.1 us (2%)
    psum x1, waiting for transfers between devices, on_device(): preact = lax.psum(pre_local, 'dp') + bias_enc  89.8 us
    psum x1, waiting for transfers between devices, on_device(): dact = lax.psum(dact_local, 'dp')  78.8 us
    all_to_all x1, blocking collectives, on_device(): lax.all_to_all(outgoing, 'dict', split_axis=0, concat_axis=0, tiled=True)  60.3 us
    all_to_all x1, blocking collectives, on_device(): lax.all_to_all(resid_out, 'dict', split_axis=0, concat_axis=0, tiled=True)  57.9 us
    all_to_all x1, waiting for transfers between devices, on_device(): lax.all_to_all(part, 'dict', split_axis=0, concat_axis=0, tiled=True)  52 us
    dot_general x1, matrix products, on_device(): lax.dot_general(rows_in, grad_pre, (((0,), (0,)), ((), ())), preferred_el...  11.3 us
    dot_general x1, matrix products, on_device(): lax.dot_general(activity, residual_in, (((0,), (0,)), ((), ())), preferre...  10.1 us
    dot_general x1, matrix products, on_device(): jnp.dot(activity, w_dec, preferred_element_type=jnp.float32)  9.98 us
  transfers between devices with their start and end apart: 3, of which 3 were waited for; matrix products, arithmetic and copies ran while one was open for 2% of the time, Pallas kernels for 0%

commit v1 on v0

v1 whole, which is shorter than its diff:
```python
import jax
import jax.numpy as jnp
from jax import lax
from jax.experimental import pallas as pl
from jax.experimental.pallas import tpu as pltpu
from jax.sharding import PartitionSpec as P


CHUNKS = 2
F32 = jnp.float32
BF16 = jnp.bfloat16
VMEM = pltpu.VMEM


def dot(a, b, dims=((1,), (0,))):
    return lax.dot_general(a, b, (dims, ((), ())), preferred_element_type=F32)


def after(value, *others):
    return lax.optimization_barrier((value,) + others)[0]


def ring(size, shift):
    return [(i, (i + shift) % size) for i in range(size)]


def params(mib=12):
    return pltpu.CompilerParams(vmem_limit_bytes=mib * 1024 * 1024)


def near(value):
    return pltpu.with_memory_space_constraint(value, VMEM)


def far(value):
    return pltpu.with_memory_space_constraint(value, pltpu.HBM)


def whole():
    return pl.BlockSpec(memory_space=VMEM)


def split_matmul(me, rows4, lane, half, weight, transposed, size):
    peers, _, slot_rows, inner = rows4.shape
    halves = 2 if half is None else 1
    my_peers = peers * halves // 2
    first = 0 if half is None else half * my_peers
    count = my_peers * slot_rows
    quarter = count // (size * halves)
    outer = weight.shape[0] if transposed else weight.shape[1]
    tile = min(256, outer)

    def body(me_ref, x_any, w_any, own_ref, *rest):
        sends, (acc, x_ref, w_ref, x_sem, w_sem) = rest[:-5], rest[-5:]
        x_copy = pltpu.make_async_copy(x_any.at[pl.ds(first, my_peers), lane], x_ref, x_sem)
        x_copy.start()

        def fetch(n):
            cols = pl.ds(pl.multiple_of(n * tile, tile), tile)
            source = w_any.at[cols, :] if transposed else w_any.at[:, cols]
            return pltpu.make_async_copy(source, w_ref.at[n], w_sem.at[n])

        for n in range(outer // tile):
            fetch(n).start()
        x_copy.wait()

        @pl.loop(0, outer // tile)
        def _(n):
            fetch(n).wait()
            rows = x_ref[...].reshape(count, inner)
            dims = ((1,), (1,)) if transposed else ((1,), (0,))
            acc[:, pl.ds(pl.multiple_of(n * tile, tile), tile)] = dot(rows, w_ref[n], dims)

        mine = me_ref[0]

        for h in range(halves):
            to = pl.ds(h * quarter, quarter)

            def piece(index):
                start = pl.multiple_of((index + h * size) * quarter, quarter)
                return acc[pl.ds(start, quarter), :]

            own_ref[to, :] = piece(mine)
            for shift in range(1, size):
                sends[shift - 1][to, :] = piece(lax.rem(mine + shift, size)).astype(BF16)

    return pl.pallas_call(
        body,
        in_specs=[pl.BlockSpec(memory_space=pltpu.SMEM)] + [pl.BlockSpec(memory_space=pl.ANY), pl.BlockSpec(memory_space=pltpu.HBM)],
        out_specs=[whole()] * size,
        out_shape=[jax.ShapeDtypeStruct((halves * quarter, outer), F32)]
        + [jax.ShapeDtypeStruct((halves * quarter, outer), BF16)] * (size - 1),
        scratch_shapes=[
            pltpu.VMEM((count, outer), F32),
            pltpu.VMEM((my_peers, slot_rows, inner), BF16),
            pltpu.VMEM((outer // tile, tile, inner) if transposed else (outer // tile, inner, tile), BF16),
            pltpu.SemaphoreType.DMA,
            pltpu.SemaphoreType.DMA((outer // tile,)),
        ],
        compiler_params=params(20),
        name="split_matmul",
    )(me, rows4, weight)


def assemble(me, parts, out_ref, size):
    quarter = out_ref.shape[0] // (2 * size)
    for i, part in enumerate(parts):
        owner = lax.rem(me + size - i % size, size)
        for j in range(part.shape[0] // quarter):
            index = owner + (i // size + j) * size
            to = pl.ds(pl.multiple_of(index * quarter, quarter), quarter)
            out_ref[to, :] = part[pl.ds(j * quarter, quarter), :]


def decode(me, pieces, w_dec, peers, slot_rows, lanes, lane, size):
    count = peers * slot_rows
    inner, outer = w_dec.shape
    tile = 512

    def body(me_ref, *refs):
        parts, w_ref, out_ref, act_ref = refs[:-3], refs[-3], refs[-2], refs[-1]
        step = pl.program_id(0)

        @pl.when(step == 0)
        def _():
            assemble(me_ref[0], parts, act_ref, size)

        part = dot(act_ref[...], w_ref[...]).astype(BF16)
        out_ref[...] = part.reshape(peers, 1, slot_rows, tile)

    return pl.pallas_call(
        body,
        grid=(outer // tile,),
        in_specs=[pl.BlockSpec(memory_space=pltpu.SMEM)]
        + [whole()] * len(pieces)
        + [pl.BlockSpec((inner, tile), lambda n: (0, n))],
        out_specs=[
            pl.BlockSpec((peers, 1, slot_rows, tile), lambda n: (0, lane, 0, n)),
            pl.BlockSpec((count, inner), lambda n: (0, 0)),
        ],
        out_shape=[
            pltpu.HBM((peers, lanes, slot_rows, outer), BF16),
            pltpu.HBM((count, inner), BF16),
        ],
        compiler_params=params(),
        name="decode",
    )(me, *pieces, w_dec)


def residual_rows(selector, returned, lane, x, bias_dec, scale, target, target_lane):
    peers, _, slot_rows, cols = returned.shape
    count = peers * slot_rows
    home = selector.shape[1]
    tile = 512

    def body(sel_ref, got_ref, x_ref, b_ref, *rest):
        out_ref = rest[-1]
        sel = sel_ref[...]
        rebuilt = dot(sel, got_ref[...].reshape(count, tile), ((0,), (0,))) + b_ref[...]
        residual = ((rebuilt - x_ref[...].astype(F32)) * scale).astype(BF16)
        out_ref[...] = dot(sel, residual).astype(BF16).reshape(peers, 1, slot_rows, tile)

    in_specs = [
        whole(),
        pl.BlockSpec((peers, 1, slot_rows, tile), lambda n: (0, lane, 0, n)),
        pl.BlockSpec((home, tile), lambda n: (0, n)),
        pl.BlockSpec((1, tile), lambda n: (0, n)),
    ]
    operands = [selector, returned, x, bias_dec]
    aliases = {}
    lanes = 1
    if target is not None:
        in_specs.append(pl.BlockSpec(memory_space=pltpu.HBM))
        operands.append(target)
        aliases = {4: 0}
        lanes = target.shape[1]
    return pl.pallas_call(
        body,
        grid=(cols // tile,),
        in_specs=in_specs,
        out_specs=pl.BlockSpec((peers, 1, slot_rows, tile), lambda n: (0, target_lane, 0, n)),
        out_shape=pltpu.HBM((peers, lanes, slot_rows, cols), BF16),
        input_output_aliases=aliases,
        compiler_params=params(),
        name="residual_rows",
    )(*operands)


def outer_sum(me, left, left_lane, right, right_lane, base, size, inside):
    pieces = right_lane is None
    if left_lane is None:
        count, wide = left.shape
    else:
        count, wide = left.shape[0] * left.shape[2], left.shape[3]
    out_cols = right[0].shape[-1]
    tile = 512
    last = base is not None

    def body(me_ref, left_ref, *refs):
        right_refs = refs[: len(right)]
        out_ref = refs[len(right) + (1 if last else 0)]
        step = pl.program_id(0)
        here = pl.ds(pl.multiple_of(step * tile, tile), tile)
        lhs = left_ref[...].reshape(count, wide)
        if pieces:
            rows_ref = refs[-1]

            @pl.when(step == 0)
            def _():
                assemble(me_ref[0], right_refs, rows_ref, size)

            rhs = rows_ref[:, here]
        else:
            rhs = right_refs[0][...].reshape(count, tile)
        total = dot(lhs, rhs, ((0,), (0,)))
        if last:
            base_ref = refs[len(right)]
            more = base_ref[:, here] if inside else base_ref[...]
            out_ref[...] = (total + more).astype(BF16)
        elif inside:
            out_ref[:, here] = total
        else:
            out_ref[...] = total

    column_block = pl.BlockSpec((wide, tile), lambda n: (0, n))
    in_specs = [pl.BlockSpec(memory_space=pltpu.SMEM)]
    operands = [me, left]
    if left_lane is None:
        in_specs.append(pl.BlockSpec((count, wide), lambda n: (0, 0)))
    else:
        operands[1] = near(left)
        in_specs.append(whole())
    if pieces:
        in_specs += [whole()] * len(right)
    else:
        peers, _, slot_rows, _ = right[0].shape
        in_specs.append(
            pl.BlockSpec((peers, 1, slot_rows, tile), lambda n: (0, right_lane, 0, n))
        )
    operands += right
    if last:
        operands.append(near(base) if inside else base)
        in_specs.append(whole() if inside else column_block)
    if last:
        out_shape = jax.ShapeDtypeStruct((wide, out_cols), BF16)
    else:
        out_shape = (VMEM if inside else pltpu.HBM)((wide, out_cols), F32)
    return pl.pallas_call(
        body,
        grid=(out_cols // tile,),
        in_specs=in_specs,
        out_specs=whole() if inside and not last else column_block,
        out_shape=out_shape,
        scratch_shapes=[pltpu.VMEM((count, out_cols), BF16)] if pieces else [],
        compiler_params=params(24),
        name="outer_sum",
    )(*operands)


def dispatch(selector, x, peers):
    out = dot(selector, x).astype(BF16)
    return out.reshape(peers, 1, out.shape[0] // peers, out.shape[1])


def exchange(rows4):
    peers, lanes, slot_rows, cols = rows4.shape
    flat = rows4.reshape(peers, lanes * slot_rows, cols)
    got = lax.all_to_all(flat, "dict", split_axis=0, concat_axis=0, tiled=True)
    return got.reshape(rows4.shape)


def swap_pieces(pieces, size):
    out = [pieces[0]]
    for shift in range(1, size):
        out.append(lax.ppermute(pieces[shift], "dp", ring(size, shift)))
    return out


def total_of(refs):
    total = refs[0][...]
    for ref in refs[1:]:
        total = total + ref[...].astype(F32)
    return total


def activate(pieces, bias_enc):
    def body(*refs):
        gate_ref, act_ref = refs[-2:]
        gate = jnp.maximum(total_of(refs[:-3]) + refs[-3][...], 0.0)
        gate_ref[...] = gate
        act_ref[...] = (gate * gate).astype(BF16)

    shape = pieces[0].shape
    return pl.pallas_call(
        body,
        in_specs=[whole()] * (len(pieces) + 1),
        out_specs=[pl.BlockSpec(shape, lambda: (0, 0)), whole()],
        out_shape=[pltpu.HBM(shape, F32), jax.ShapeDtypeStruct(shape, BF16)],
        compiler_params=params(),
        name="activate",
    )(*pieces, bias_enc)


def grad_pre(pieces, gates, start):
    rows = pieces[0].shape[0]
    size = len(pieces)

    def body(*refs):
        total = total_of(refs[:size])
        done = 0
        for ref in refs[size:-1]:
            count = min(rows - done, ref.shape[0])
            part = total[done : done + count] * 2.0 * ref[pl.ds(start, count), :]
            refs[-1][pl.ds(done, count), :] = part.astype(BF16)
            done += count

    return pl.pallas_call(
        body,
        in_specs=[whole()] * (size + len(gates)),
        out_specs=whole(),
        out_shape=jax.ShapeDtypeStruct(pieces[0].shape, BF16),
        compiler_params=params(),
        name="grad_pre",
    )(*pieces, *gates)


def spread(own, size):
    out = [own]
    for shift in range(1, size):
        out.append(lax.ppermute(own, "dp", ring(size, shift)))
    return out


def on_device(acts, lists, w_enc, w_dec, b_enc, b_dec):
    peers = lax.axis_size("dict")
    size = lax.axis_size("dp")
    me = lax.axis_index("dp").reshape(1).astype(jnp.int32)
    block_count, active_count = lists.shape
    rows_block = acts.shape[0] // block_count
    cols = acts.shape[1]
    capacity = max(2, (2 * block_count * active_count + peers - 1) // peers)
    slot_total = peers * capacity
    sub = rows_block // CHUNKS
    slot_rows = capacity * sub

    flat_ids = lists.reshape(-1)
    onehot = (flat_ids[:, None] == jnp.arange(peers, dtype=jnp.int32)[None, :]).astype(jnp.int32)
    rank_index = jnp.sum((jnp.cumsum(onehot, axis=0) - 1) * onehot, axis=1)
    slot_index = flat_ids * capacity + rank_index
    item_block = jnp.arange(block_count * active_count, dtype=jnp.int32) // active_count
    hit = jnp.arange(slot_total, dtype=jnp.int32)[:, None] == slot_index[None, :]
    slot_block = jnp.sum(jnp.where(hit, item_block[None, :] + 1, 0), axis=1) - 1
    slot_row = slot_block[:, None] * sub + jnp.arange(sub, dtype=jnp.int32)[None, :]
    slot_row = jnp.where(slot_block[:, None] >= 0, slot_row, -1).reshape(-1)
    selector = (
        slot_row[:, None] == jnp.arange(block_count * sub, dtype=jnp.int32)[None, :]
    ).astype(BF16)

    blocks = acts.reshape(block_count, CHUNKS, sub, cols)
    x_a = blocks[:, 0].reshape(block_count * sub, cols)
    x_b = blocks[:, 1].reshape(block_count * sub, cols)
    bias_enc = b_enc.astype(F32).reshape(1, -1)
    bias_dec = b_dec.astype(F32).reshape(1, cols)
    scale = 1.0 / rows_block
    w_enc = far(w_enc)
    w_dec = far(w_dec)

    def share(rows4, lane, half, weight, transposed):
        return split_matmul(me, rows4, lane, half, weight, transposed, size)


    in_a = exchange(dispatch(selector, x_a, peers))
    in_b = exchange(after(dispatch(selector, x_b, peers), in_a))
    gates_a, own_a = [], []
    for h in range(2):
        pieces = share(in_a, 0, h, w_enc, False)
        pieces = swap_pieces(pieces, size)
        gate, act = activate(pieces, bias_enc)
        gates_a.append(gate)
        own_a.append(act)
    pieces_a = spread(own_a[0], size) + spread(own_a[1], size)
    enc_b = share(in_b, 0, None, w_enc, False)
    enc_b = swap_pieces(enc_b, size)
    part_a, act_a = decode(me, pieces_a, w_dec, peers, slot_rows, 1, 0, size)
    back_a = exchange(part_a)
    gate_b, own_b = activate(enc_b, bias_enc)
    pieces_b = spread(own_b, size)
    part_b, act_b = decode(me, pieces_b, w_dec, peers, slot_rows, 2, 0, size)
    mixed = residual_rows(selector, back_a, 0, x_a, bias_dec, scale, part_b, 1)
    mixed = far(exchange(mixed))
    resid_b = residual_rows(selector, mixed, 0, x_b, bias_dec, scale, None, 0)
    last = exchange(resid_b)
    back = share(mixed, 1, None, w_dec, True)
    back = swap_pieces(back, size)
    dec_sum = outer_sum(me, act_a, None, [mixed], 1, None, size, False)
    gp_a = grad_pre(back, gates_a, 0)
    pre_a = spread(gp_a, size)
    backs = []
    for h in range(2):
        pieces = share(last, 0, h, w_dec, True)
        backs.append(swap_pieces(pieces, size))
    enc_sum = outer_sum(me, in_a, 0, pre_a, None, None, size, True)
    half = gate_b.shape[0] // 2
    pre_b = []
    for h in range(2):
        pieces = backs[h]
        if h == 0:
            pieces[0] = after(pieces[0], enc_sum)
        gp_b = grad_pre(pieces, [gate_b], h * half)
        pre_b += spread(gp_b, size)
    grad_dec = outer_sum(me, act_b, None, [last], 0, dec_sum, size, False)
    grad_enc = outer_sum(me, in_b, 0, pre_b, None, enc_sum, size, True)
    return grad_enc, grad_dec


def solution(mesh):
    in_specs = (
        P("dict", "dp"),
        P("dict", None),
        P("dp", "dict"),
        P("dict", "dp"),
        P("dict"),
        P("dp"),
    )
    out_specs = (P("dp", "dict"), P("dict", "dp"))
    return jax.shard_map(
        on_device, mesh=mesh, in_specs=in_specs, out_specs=out_specs, check_vma=False
    )
```

time: 450 us -> 292 us (0.65); the launches traced: 450 us -> 287 us
  waiting for transfers between devices: 221 us -> 80.6 us
  Pallas kernels: 0 us -> 67.5 us
  starting transfers between devices: 8.1 us -> 69.2 us
  blocking collectives: 118 us -> 58.5 us
  matrix products: 54.5 us -> 5.19 us
  local copies, waits for them, and re-layouts: 32.4 us -> 4.53 us
  between operations: 14.1 us -> 0.98 us
    psum x2 -> x0, waiting for transfers between devices: 169 us -> none  [the longest x1 89.8 us: on_device(): preact = lax.psum(pre_local, 'dp') + bias_enc]
    pallas_call x0 -> x20, Pallas kernels: none -> 67.5 us  [the longest x6 24.3 us: split_matmul(): pl.pallas_call(body, in_specs=[pl.BlockSpec(memory_space=pltpu.SMEM)] + [...]
    all_to_all x2 -> x1, blocking collectives: 118 us -> 58.5 us  [exchange(): got = lax.all_to_all(flat, 'dict', split_axis=0, concat_axis=0, tiled=True)]
    ppermute x0 -> x36, waiting for transfers between devices: none -> 50.1 us  [the longest x18 29 us: swap_pieces(): out.append(lax.ppermute(pieces[shift], 'dp', ring(size, shift)))]
    dot_general x9 -> x2, matrix products: 54.5 us -> 5.19 us  [dot(): return lax.dot_general(a, b, (dims, ((), ())), preferred_element_type=F32)]
    ppermute x0 -> x36, starting transfers between devices: none -> 40.6 us  [the longest x18 21.2 us: swap_pieces(): out.append(lax.ppermute(pieces[shift], 'dp', ring(size, shift)))]
    reshape x6 -> x0, local copies, waits for them, and re-layouts: 26.9 us -> none  [the longest x1 7.37 us: on_device(): returned = returned.reshape(slot_total, rows_block * feature_cols)]
    all_to_all x1 -> x4, waiting for transfers between devices: 52 us -> 30.4 us  [exchange(): got = lax.all_to_all(flat, 'dict', split_axis=0, concat_axis=0, tiled=True)]
  transfers between devices with their start and end apart: 3 -> 40, of which waited for: 3 -> 18; matrix products, arithmetic and copies ran while one was open for 2% -> 1% of each run, Pallas kernels for 0% -> 19%
where the time goes in v1:
time: 292 us; the launch traced here: 287 us
  waiting for transfers between devices  80.6 us (28%)
  starting transfers between devices  69.2 us (24%)
  Pallas kernels  67.5 us (23%)
  blocking collectives  58.5 us (20%)
  matrix products  5.19 us (2%)
  local copies, waits for them, and re-layouts  4.53 us (2%)
    all_to_all x1, blocking collectives, exchange(): got = lax.all_to_all(flat, 'dict', split_axis=0, concat_axis=0, tiled=True)  58.5 us
    all_to_all x4, waiting for transfers between devices, exchange(): got = lax.all_to_all(flat, 'dict', split_axis=0, concat_axis=0, tiled=True)  30.4 us
    ppermute x18, waiting for transfers between devices, swap_pieces(): out.append(lax.ppermute(pieces[shift], 'dp', ring(size, shift)))  29 us
    all_to_all x4, starting transfers between devices, exchange(): got = lax.all_to_all(flat, 'dict', split_axis=0, concat_axis=0, tiled=True)  28.7 us
    pallas_call x6, Pallas kernels, split_matmul(): pl.pallas_call(body, in_specs=[pl.BlockSpec(memory_space=pltpu.SMEM)] + [...  24.3 us
    ppermute x18, starting transfers between devices, swap_pieces(): out.append(lax.ppermute(pieces[shift], 'dp', ring(size, shift)))  21.2 us
    ppermute x18, waiting for transfers between devices, spread(): out.append(lax.ppermute(own, 'dp', ring(size, shift)))  21.1 us
    pallas_call x4, Pallas kernels, outer_sum(): pl.pallas_call(body, grid=(out_cols // tile,), in_specs=in_specs, out_spe...  20.3 us
  transfers between devices with their start and end apart: 40, of which 18 were waited for; matrix products, arithmetic and copies ran while one was open for 1% of the time, Pallas kernels for 19%

profile of v1, /device:TPU:1, one launch (start us, length us, event | category | flops | bytes accessed | tf_op | source)
XLA Modules:
  0.0 287.1 jit_solution(16033436157900184454)
XLA Ops:
  5.3 9.4 %all-to-all-start = ((bf16[32,16,2048]{2,1,0:T(8,128)(2,1)}), bf16[32,16,2048]{2,1,0:T(8,128)(2,1)S(1)}, u32[]{:S(2)}, u32[]{:S(2)}) async-start(bf16[32,16,2048]{2,1,0:T(8,128)(2,1)} %bitcast.42), calls=%async_computation | async-start | bytes 4194304 | tf_op jit(solution)/shard_map/all_to_all | solution.py:268
  16.8 26.3 %all-to-all-done = bf16[32,16,2048]{2,1,0:T(8,128)(2,1)S(1)} async-done(((bf16[32,16,2048]{2,1,0:T(8,128)(2,1)}), bf16[32,16,2048]{2,1,0:T(8,128)(2,1)S(1)}, u32[]{:S(2)}, u32[]{:S(2)}) %all-to-all-start) | async-done | bytes 2097184 | tf_op jit(solution)/shard_map/all_to_all | solution.py:268
  43.1 5.2 %all-to-all-start.1 = ((bf16[32,16,2048]{2,1,0:T(8,128)(2,1)}), bf16[32,16,2048]{2,1,0:T(8,128)(2,1)}, u32[]{:S(2)}, u32[]{:S(2)}) async-start(bf16[32,16,2048]{2,1,0:T(8,128)(2,1)} %bitcast.41), calls=%async_computation.1 | async-start | bytes 4194304 | tf_op jit(solution)/shard_map/all_to_all | solution.py:268
  69.0 3.5 %collective-permute-start.5 = (bf16[64,1024]{1,0:T(8,128)(2,1)S(1)}, bf16[64,1024]{1,0:T(8,128)(2,1)S(1)}, u32[]{:S(2)}, u32[]{:S(2)}) collective-permute-start(bf16[64,1024]{1,0:T(8,128)(2,1)S(1)} %get-tuple-element.43.refs_0_), channel_id=1, source_target_pairs={{0,96},{32,0},{64,32},{96,64},{1,97},{33,1},{65,33},{97,65},{2,98}... | collective-permute-start | bytes 393224 | tf_op jit(solution)/shard_map/ppermute | solution.py:330
  79.9 5.8 %decode.2 = (bf16[32,1,16,2048]{3,2,1,0:T(8,128)(2,1)}, bf16[512,1024]{1,0:T(8,128)(2,1)}) custom-call(s32[1]{0:T(128)} %bitcast.me_ref, bf16[64,1024]{1,0:T(8,128)(2,1)S(1)} %get-tuple-element.43.refs_0_, bf16[64,1024]{1,0:T(8,128)(2,1)S(1)} %collective-permute-done.3.refs_1_, bf16[64,1024]{1,0:T(8,128)(2,1)S(1)} %collective-permute-done.4.refs_2_, ...), custom_call_target="tpu_custom_call" | custom-call | tf_op jit(solution)/shard_map/decode/pallas_call | solution.py:131
  85.6 10.1 %all-to-all-start.2 = ((bf16[32,16,2048]{2,1,0:T(8,128)(2,1)}), bf16[32,16,2048]{2,1,0:T(8,128)(2,1)S(1)}, u32[]{:S(2)}, u32[]{:S(2)}) async-start(bf16[32,16,2048]{2,1,0:T(8,128)(2,1)} %bitcast.47), calls=%async_computation.2 | async-start | bytes 4194304 | tf_op jit(solution)/shard_map/all_to_all | solution.py:268
  95.8 5.7 %split_matmul.8 = (f32[128,1024]{1,0:T(8,128)S(1)}, bf16[128,1024]{1,0:T(8,128)(2,1)S(1)}, bf16[128,1024]{1,0:T(8,128)(2,1)S(1)}, bf16[128,1024]{1,0:T(8,128)(2,1)S(1)}) custom-call(s32[1]{0:T(128)} %bitcast.me_ref, bf16[32,1,16,2048]{3,2,1,0:T(8,128)(2,1)} %bitcast.8.x_any.left_ref, bf16[2048,1024]{1,0:T(8,128)(2,1)} %w_any.8), custom_call_target="tpu_custom_call" | custom-call | tf_op jit(solution)/shard_map/split_matmul/pallas_call | solution.py:87
  104.2 6.6 %collective-permute-done.12.refs_1_ = bf16[128,1024]{1,0:T(8,128)(2,1)S(1)} collective-permute-done((bf16[128,1024]{1,0:T(8,128)(2,1)S(1)}, bf16[128,1024]{1,0:T(8,128)(2,1)S(1)}, u32[]{:S(2)}, u32[]{:S(2)}) %collective-permute-start.12) | collective-permute-done | bytes 262176 | tf_op jit(solution)/shard_map/ppermute | solution.py:275
  110.8 4.8 %collective-permute-done.13.refs_2_ = bf16[128,1024]{1,0:T(8,128)(2,1)S(1)} collective-permute-done((bf16[128,1024]{1,0:T(8,128)(2,1)S(1)}, bf16[128,1024]{1,0:T(8,128)(2,1)S(1)}, u32[]{:S(2)}, u32[]{:S(2)}) %collective-permute-start.13) | collective-permute-done | bytes 262176 | tf_op jit(solution)/shard_map/ppermute | solution.py:275
  120.8 5.6 %collective-permute-done.17.refs_3_ = bf16[128,1024]{1,0:T(8,128)(2,1)S(1)} collective-permute-done((bf16[128,1024]{1,0:T(8,128)(2,1)S(1)}, bf16[128,1024]{1,0:T(8,128)(2,1)S(1)}, u32[]{:S(2)}, u32[]{:S(2)}) %collective-permute-start.17) | collective-permute-done | bytes 262176 | tf_op jit(solution)/shard_map/ppermute | solution.py:330
  128.3 6.4 %collective-permute-done.15.refs_1_ = bf16[128,1024]{1,0:T(8,128)(2,1)S(1)} collective-permute-done((bf16[128,1024]{1,0:T(8,128)(2,1)S(1)}, bf16[128,1024]{1,0:T(8,128)(2,1)S(1)}, u32[]{:S(2)}, u32[]{:S(2)}) %collective-permute-start.15) | collective-permute-done | bytes 262176 | tf_op jit(solution)/shard_map/ppermute | solution.py:330
  134.7 6.2 %decode.3 = (bf16[32,2,16,2048]{3,2,1,0:T(8,128)(2,1)}, bf16[512,1024]{1,0:T(8,128)(2,1)}) custom-call(s32[1]{0:T(128)} %bitcast.me_ref, bf16[128,1024]{1,0:T(8,128)(2,1)S(1)} %get-tuple-element.54.refs_0_, bf16[128,1024]{1,0:T(8,128)(2,1)S(1)} %collective-permute-done.15.refs_1_, bf16[128,1024]{1,0:T(8,128)(2,1)S(1)} %collective-permute-done.16.refs_2_, ...), custom_call_target="tpu_custom_call" | custom-call | tf_op jit(solution)/shard_map/decode/pallas_call | solution.py:131
  140.9 3.3 %residual_rows.2 = bf16[32,2,16,2048]{3,2,1,0:T(8,128)(2,1)} custom-call(bf16[512,128]{1,0:T(8,128)(2,1)S(1)} %fusion.sel_ref, bf16[32,1,16,2048]{3,2,1,0:T(8,128)(2,1)S(1)} %bitcast.31, bf16[128,2048]{1,0:T(8,128)(2,1)S(1)} %get-tuple-element.75.x_ref, f32[1,2048]{1,0:T(1,128)S(1)} %bitcast.32, ...), custom_call_target="tpu_custom_call", output_to_operand_aliasing={{}: (4, {})} | custom-call | tf_op jit(solution)/shard_map/residual_rows/pallas_call | solution.py:177
  144.2 58.5 %all_to_all.25 = bf16[32,32,2048]{2,1,0:T(8,128)(2,1)} all-to-all(bf16[32,32,2048]{2,1,0:T(8,128)(2,1)} %bitcast.40), channel_id=1, replica_groups=mesh['dp'=4,'dict'=32] {'dict'}, dimensions={0} | all-to-all | bytes 8388608 | tf_op jit(solution)/shard_map/all_to_all | solution.py:268
  202.7 4.8 %residual_rows.3 = bf16[32,1,16,2048]{3,2,1,0:T(8,128)(2,1)} custom-call(bf16[512,128]{1,0:T(8,128)(2,1)S(1)} %fusion.sel_ref, bf16[32,2,16,2048]{3,2,1,0:T(8,128)(2,1)} %bitcast.37, bf16[128,2048]{1,0:T(8,128)(2,1)S(1)} %get-tuple-element.74.x_ref, f32[1,2048]{1,0:T(1,128)S(1)} %bitcast.33), custom_call_target="tpu_custom_call" | custom-call | tf_op jit(solution)/shard_map/residual_rows/pallas_call | solution.py:177
  207.5 3.9 %all-to-all-start.4 = ((bf16[32,16,2048]{2,1,0:T(8,128)(2,1)}), bf16[32,16,2048]{2,1,0:T(8,128)(2,1)S(1)}, u32[]{:S(2)}, u32[]{:S(2)}) async-start(bf16[32,16,2048]{2,1,0:T(8,128)(2,1)} %bitcast.43), calls=%async_computation.4 | async-start | bytes 4194304 | tf_op jit(solution)/shard_map/all_to_all | solution.py:268
  211.4 5.7 %split_matmul.10 = (f32[128,1024]{1,0:T(8,128)S(1)}, bf16[128,1024]{1,0:T(8,128)(2,1)S(1)}, bf16[128,1024]{1,0:T(8,128)(2,1)S(1)}, bf16[128,1024]{1,0:T(8,128)(2,1)S(1)}) custom-call(s32[1]{0:T(128)} %bitcast.me_ref, bf16[32,2,16,2048]{3,2,1,0:T(8,128)(2,1)} %bitcast.38, bf16[1024,2048]{1,0:T(8,128)(2,1)} %w_any.11), custom_call_target="tpu_custom_call" | custom-call | tf_op jit(solution)/shard_map/split_matmul/pallas_call | solution.py:87
  219.9 11.8 %collective-permute-done.18.refs_1_ = bf16[128,1024]{1,0:T(8,128)(2,1)S(1)} collective-permute-done((bf16[128,1024]{1,0:T(8,128)(2,1)S(1)}, bf16[128,1024]{1,0:T(8,128)(2,1)S(1)}, u32[]{:S(2)}, u32[]{:S(2)}) %collective-permute-start.18) | collective-permute-done | bytes 262176 | tf_op jit(solution)/shard_map/ppermute | solution.py:275
  235.6 4.2 %all-to-all-done.4 = bf16[32,16,2048]{2,1,0:T(8,128)(2,1)S(1)} async-done(((bf16[32,16,2048]{2,1,0:T(8,128)(2,1)}), bf16[32,16,2048]{2,1,0:T(8,128)(2,1)S(1)}, u32[]{:S(2)}, u32[]{:S(2)}) %all-to-all-start.4) | async-done | bytes 2097184 | tf_op jit(solution)/shard_map/all_to_all | solution.py:268
  244.9 3.9 %collective-permute-start.32 = (bf16[64,1024]{1,0:T(8,128)(2,1)S(1)}, bf16[64,1024]{1,0:T(8,128)(2,1)S(1)}, u32[]{:S(2)}, u32[]{:S(2)}) collective-permute-start(bf16[64,1024]{1,0:T(8,128)(2,1)S(1)} %get-tuple-element.71), channel_id=1, source_target_pairs={{0,96},{32,0},{64,32},{96,64},{1,97},{33,1},{65,33},{97,65},{2,98}... | collective-permute-start | bytes 393224 | tf_op jit(solution)/shard_map/ppermute | solution.py:275
  266.3 6.7 %outer_sum.6.refs_1_ = f32[1024,2048]{1,0:T(8,128)} custom-call(s32[1]{0:T(128)} %bitcast.me_ref, bf16[512,1024]{1,0:T(8,128)(2,1)S(1)} %copy-done.5, bf16[32,2,16,2048]{3,2,1,0:T(8,128)(2,1)} %bitcast.39), custom_call_target="tpu_custom_call" | custom-call | tf_op jit(solution)/shard_map/outer_sum/pallas_call | solution.py:248
  273.0 3.4 %copy-done = f32[1024,2048]{1,0:T(8,128)S(1)} copy-done((f32[1024,2048]{1,0:T(8,128)S(1)}, f32[1024,2048]{1,0:T(8,128)}, u32[]{:S(2)}) %copy-start) | copy-done | bytes 8388632
  276.4 4.7 %outer_sum.7 = bf16[1024,2048]{1,0:T(8,128)(2,1)} custom-call(s32[1]{0:T(128)} %bitcast.me_ref, bf16[512,1024]{1,0:T(8,128)(2,1)S(1)} %copy-done.4, bf16[32,1,16,2048]{3,2,1,0:T(8,128)(2,1)S(1)} %bitcast.27, f32[1024,2048]{1,0:T(8,128)S(1)} %copy-done), custom_call_target="tpu_custom_call" | custom-call | tf_op jit(solution)/shard_map/outer_sum/pallas_call | solution.py:248
  281.2 5.9 %outer_sum.5 = bf16[2048,1024]{1,0:T(8,128)(2,1)} custom-call(s32[1]{0:T(128)} %bitcast.me_ref, bf16[32,1,16,2048]{3,2,1,0:T(8,128)(2,1)} %bitcast.8.x_any.left_ref, bf16[64,1024]{1,0:T(8,128)(2,1)S(1)} %grad_pre.4.refs_0_, bf16[64,1024]{1,0:T(8,128)(2,1)S(1)} %collective-permute-done.27.refs_1_, bf16[64,1024]{1,0:T(8,128)(2,1)S(1)} %collective-permute-done.28.refs_2_, ...), custom_call_target="tpu_custom_call" | custom-call | tf_op jit(solution)/shard_map/outer_sum/pallas_call | solution.py:248
  (118 shorter events, 73.8 us)
Async XLA Ops:
  5.3 37.8 %all-to-all-start = ((bf16[32,16,2048]{2,1,0:T(8,128)(2,1)}), bf16[32,16,2048]{2,1,0:T(8,128)(2,1)S(1)}, u32[]{:S(2)}, u32[]{:S(2)}) async-start(bf16[32,16,2048]{2,1,0:T(8,128)(2,1)} %bitcast.42), calls=%async_computation | async-start | bytes 4194304 | tf_op jit(solution)/shard_map/all_to_all | solution.py:268
  43.1 42.5 %all-to-all-start.1 = ((bf16[32,16,2048]{2,1,0:T(8,128)(2,1)}), bf16[32,16,2048]{2,1,0:T(8,128)(2,1)}, u32[]{:S(2)}, u32[]{:S(2)}) async-start(bf16[32,16,2048]{2,1,0:T(8,128)(2,1)} %bitcast.41), calls=%async_computation.1 | async-start | bytes 4194304 | tf_op jit(solution)/shard_map/all_to_all | solution.py:268
  51.5 9.5 %collective-permute-start.6 = (bf16[64,1024]{1,0:T(8,128)(2,1)S(1)}, bf16[64,1024]{1,0:T(8,128)(2,1)S(1)}, u32[]{:S(2)}, u32[]{:S(2)}) collective-permute-start(bf16[64,1024]{1,0:T(8,128)(2,1)S(1)} %get-tuple-element.45), channel_id=1, source_target_pairs={{0,32},{32,64},{64,96},{96,0},{1,33},{33,65},{65,97},{97,1},{2,34}... | collective-permute-start | bytes 393224 | tf_op jit(solution)/shard_map/ppermute | solution.py:275
  52.8 9.8 %collective-permute-start.7 = (bf16[64,1024]{1,0:T(8,128)(2,1)S(1)}, bf16[64,1024]{1,0:T(8,128)(2,1)S(1)}, u32[]{:S(2)}, u32[]{:S(2)}) collective-permute-start(bf16[64,1024]{1,0:T(8,128)(2,1)S(1)} %get-tuple-element.46), channel_id=1, source_target_pairs={{0,64},{32,96},{64,0},{96,32},{1,65},{33,97},{65,1},{97,33},{2,66}... | collective-permute-start | bytes 393224 | tf_op jit(solution)/shard_map/ppermute | solution.py:275
  85.6 55.2 %all-to-all-start.2 = ((bf16[32,16,2048]{2,1,0:T(8,128)(2,1)}), bf16[32,16,2048]{2,1,0:T(8,128)(2,1)S(1)}, u32[]{:S(2)}, u32[]{:S(2)}) async-start(bf16[32,16,2048]{2,1,0:T(8,128)(2,1)} %bitcast.47), calls=%async_computation.2 | async-start | bytes 4194304 | tf_op jit(solution)/shard_map/all_to_all | solution.py:268
  101.6 14.0 %collective-permute-start.13 = (bf16[128,1024]{1,0:T(8,128)(2,1)S(1)}, bf16[128,1024]{1,0:T(8,128)(2,1)S(1)}, u32[]{:S(2)}, u32[]{:S(2)}) collective-permute-start(bf16[128,1024]{1,0:T(8,128)(2,1)S(1)} %get-tuple-element.52), channel_id=1, source_target_pairs={{0,64},{32,96},{64,0},{96,32},{1,65},{33,97},{65,1},{97,33},{2,66}... | collective-permute-start | bytes 786440 | tf_op jit(solution)/shard_map/ppermute | solution.py:275
  103.8 12.6 %collective-permute-start.14 = (bf16[128,1024]{1,0:T(8,128)(2,1)S(1)}, bf16[128,1024]{1,0:T(8,128)(2,1)S(1)}, u32[]{:S(2)}, u32[]{:S(2)}) collective-permute-start(bf16[128,1024]{1,0:T(8,128)(2,1)S(1)} %get-tuple-element.53), channel_id=1, source_target_pairs={{0,96},{32,0},{64,32},{96,64},{1,97},{33,1},{65,33},{97,65},{2,98}... | collective-permute-start | bytes 786440 | tf_op jit(solution)/shard_map/ppermute | solution.py:275
  119.9 14.8 %collective-permute-start.15 = (bf16[128,1024]{1,0:T(8,128)(2,1)S(1)}, bf16[128,1024]{1,0:T(8,128)(2,1)S(1)}, u32[]{:S(2)}, u32[]{:S(2)}) collective-permute-start(bf16[128,1024]{1,0:T(8,128)(2,1)S(1)} %get-tuple-element.54.refs_0_), channel_id=1, source_target_pairs={{0,32},{32,64},{64,96},{96,0},{1,33},{33,65},{65,97},{97,1},{2,34}... | collective-permute-start | bytes 786440 | tf_op jit(solution)/shard_map/ppermute | solution.py:330
  207.5 32.3 %all-to-all-start.4 = ((bf16[32,16,2048]{2,1,0:T(8,128)(2,1)}), bf16[32,16,2048]{2,1,0:T(8,128)(2,1)S(1)}, u32[]{:S(2)}, u32[]{:S(2)}) async-start(bf16[32,16,2048]{2,1,0:T(8,128)(2,1)} %bitcast.43), calls=%async_computation.4 | async-start | bytes 4194304 | tf_op jit(solution)/shard_map/all_to_all | solution.py:268
  217.2 14.5 %collective-permute-start.18 = (bf16[128,1024]{1,0:T(8,128)(2,1)S(1)}, bf16[128,1024]{1,0:T(8,128)(2,1)S(1)}, u32[]{:S(2)}, u32[]{:S(2)}) collective-permute-start(bf16[128,1024]{1,0:T(8,128)(2,1)S(1)} %get-tuple-element.58), channel_id=1, source_target_pairs={{0,32},{32,64},{64,96},{96,0},{1,33},{33,65},{65,97},{97,1},{2,34}... | collective-permute-start | bytes 786440 | tf_op jit(solution)/shard_map/ppermute | solution.py:275
  217.3 14.4 %collective-permute-start.19 = (bf16[128,1024]{1,0:T(8,128)(2,1)S(1)}, bf16[128,1024]{1,0:T(8,128)(2,1)S(1)}, u32[]{:S(2)}, u32[]{:S(2)}) collective-permute-start(bf16[128,1024]{1,0:T(8,128)(2,1)S(1)} %get-tuple-element.59), channel_id=1, source_target_pairs={{0,64},{32,96},{64,0},{96,32},{1,65},{33,97},{65,1},{97,33},{2,66}... | collective-permute-start | bytes 786440 | tf_op jit(solution)/shard_map/ppermute | solution.py:275
  219.0 13.0 %collective-permute-start.20 = (bf16[128,1024]{1,0:T(8,128)(2,1)S(1)}, bf16[128,1024]{1,0:T(8,128)(2,1)S(1)}, u32[]{:S(2)}, u32[]{:S(2)}) collective-permute-start(bf16[128,1024]{1,0:T(8,128)(2,1)S(1)} %get-tuple-element.60), channel_id=1, source_target_pairs={{0,96},{32,0},{64,32},{96,64},{1,97},{33,1},{65,33},{97,65},{2,98}... | collective-permute-start | bytes 786440 | tf_op jit(solution)/shard_map/ppermute | solution.py:275
  232.2 12.7 %collective-permute-start.23 = (bf16[128,1024]{1,0:T(8,128)(2,1)S(1)}, bf16[128,1024]{1,0:T(8,128)(2,1)S(1)}, u32[]{:S(2)}, u32[]{:S(2)}) collective-permute-start(bf16[128,1024]{1,0:T(8,128)(2,1)S(1)} %grad_pre.3.refs_0_), channel_id=1, source_target_pairs={{0,96},{32,0},{64,32},{96,64},{1,97},{33,1},{65,33},{97,65},{2,98}... | collective-permute-start | bytes 786440 | tf_op jit(solution)/shard_map/ppermute | solution.py:330
  234.9 21.4 %collective-permute-start.22 = (bf16[128,1024]{1,0:T(8,128)(2,1)S(1)}, bf16[128,1024]{1,0:T(8,128)(2,1)S(1)}, u32[]{:S(2)}, u32[]{:S(2)}) collective-permute-start(bf16[128,1024]{1,0:T(8,128)(2,1)S(1)} %grad_pre.3.refs_0_), channel_id=1, source_target_pairs={{0,64},{32,96},{64,0},{96,32},{1,65},{33,97},{65,1},{97,33},{2,66}... | collective-permute-start | bytes 786440 | tf_op jit(solution)/shard_map/ppermute | solution.py:330
  234.9 22.8 %collective-permute-start.21 = (bf16[128,1024]{1,0:T(8,128)(2,1)S(1)}, bf16[128,1024]{1,0:T(8,128)(2,1)S(1)}, u32[]{:S(2)}, u32[]{:S(2)}) collective-permute-start(bf16[128,1024]{1,0:T(8,128)(2,1)S(1)} %grad_pre.3.refs_0_), channel_id=1, source_target_pairs={{0,32},{32,64},{64,96},{96,0},{1,33},{33,65},{65,97},{97,1},{2,34}... | collective-permute-start | bytes 786440 | tf_op jit(solution)/shard_map/ppermute | solution.py:330
  243.1 10.2 %collective-permute-start.30 = (bf16[64,1024]{1,0:T(8,128)(2,1)S(1)}, bf16[64,1024]{1,0:T(8,128)(2,1)S(1)}, u32[]{:S(2)}, u32[]{:S(2)}) collective-permute-start(bf16[64,1024]{1,0:T(8,128)(2,1)S(1)} %get-tuple-element.69), channel_id=1, source_target_pairs={{0,32},{32,64},{64,96},{96,0},{1,33},{33,65},{65,97},{97,1},{2,34}... | collective-permute-start | bytes 393224 | tf_op jit(solution)/shard_map/ppermute | solution.py:275
  243.2 11.1 %collective-permute-start.31 = (bf16[64,1024]{1,0:T(8,128)(2,1)S(1)}, bf16[64,1024]{1,0:T(8,128)(2,1)S(1)}, u32[]{:S(2)}, u32[]{:S(2)}) collective-permute-start(bf16[64,1024]{1,0:T(8,128)(2,1)S(1)} %get-tuple-element.70), channel_id=1, source_target_pairs={{0,64},{32,96},{64,0},{96,32},{1,65},{33,97},{65,1},{97,33},{2,66}... | collective-permute-start | bytes 393224 | tf_op jit(solution)/shard_map/ppermute | solution.py:275
  244.9 9.8 %collective-permute-start.32 = (bf16[64,1024]{1,0:T(8,128)(2,1)S(1)}, bf16[64,1024]{1,0:T(8,128)(2,1)S(1)}, u32[]{:S(2)}, u32[]{:S(2)}) collective-permute-start(bf16[64,1024]{1,0:T(8,128)(2,1)S(1)} %get-tuple-element.71), channel_id=1, source_target_pairs={{0,96},{32,0},{64,32},{96,64},{1,97},{33,1},{65,33},{97,65},{2,98}... | collective-permute-start | bytes 393224 | tf_op jit(solution)/shard_map/ppermute | solution.py:275
  256.4 9.6 %collective-permute-start.35 = (bf16[64,1024]{1,0:T(8,128)(2,1)S(1)}, bf16[64,1024]{1,0:T(8,128)(2,1)S(1)}, u32[]{:S(2)}, u32[]{:S(2)}) collective-permute-start(bf16[64,1024]{1,0:T(8,128)(2,1)S(1)} %grad_pre.5.refs_4_), channel_id=1, source_target_pairs={{0,96},{32,0},{64,32},{96,64},{1,97},{33,1},{65,33},{97,65},{2,98}... | collective-permute-start | bytes 393224 | tf_op jit(solution)/shard_map/ppermute | solution.py:330
  260.6 20.5 %collective-permute-start.34 = (bf16[64,1024]{1,0:T(8,128)(2,1)S(1)}, bf16[64,1024]{1,0:T(8,128)(2,1)S(1)}, u32[]{:S(2)}, u32[]{:S(2)}) collective-permute-start(bf16[64,1024]{1,0:T(8,128)(2,1)S(1)} %grad_pre.5.refs_4_), channel_id=1, source_target_pairs={{0,64},{32,96},{64,0},{96,32},{1,65},{33,97},{65,1},{97,33},{2,66}... | collective-permute-start | bytes 393224 | tf_op jit(solution)/shard_map/ppermute | solution.py:330
  261.6 19.6 %collective-permute-start.33 = (bf16[64,1024]{1,0:T(8,128)(2,1)S(1)}, bf16[64,1024]{1,0:T(8,128)(2,1)S(1)}, u32[]{:S(2)}, u32[]{:S(2)}) collective-permute-start(bf16[64,1024]{1,0:T(8,128)(2,1)S(1)} %grad_pre.5.refs_4_), channel_id=1, source_target_pairs={{0,32},{32,64},{64,96},{96,0},{1,33},{33,65},{65,97},{97,1},{2,34}... | collective-permute-start | bytes 393224 | tf_op jit(solution)/shard_map/ppermute | solution.py:330
  262.5 18.7 %collective-permute-start.29 = (bf16[64,1024]{1,0:T(8,128)(2,1)S(1)}, bf16[64,1024]{1,0:T(8,128)(2,1)S(1)}, u32[]{:S(2)}, u32[]{:S(2)}) collective-permute-start(bf16[64,1024]{1,0:T(8,128)(2,1)S(1)} %grad_pre.4.refs_0_), channel_id=1, source_target_pairs={{0,96},{32,0},{64,32},{96,64},{1,97},{33,1},{65,33},{97,65},{2,98}... | collective-permute-start | bytes 393224 | tf_op jit(solution)/shard_map/ppermute | solution.py:330
  265.6 15.5 %collective-permute-start.28 = (bf16[64,1024]{1,0:T(8,128)(2,1)S(1)}, bf16[64,1024]{1,0:T(8,128)(2,1)S(1)}, u32[]{:S(2)}, u32[]{:S(2)}) collective-permute-start(bf16[64,1024]{1,0:T(8,128)(2,1)S(1)} %grad_pre.4.refs_0_), channel_id=1, source_target_pairs={{0,64},{32,96},{64,0},{96,32},{1,65},{33,97},{65,1},{97,33},{2,66}... | collective-permute-start | bytes 393224 | tf_op jit(solution)/shard_map/ppermute | solution.py:330
  266.0 15.2 %collective-permute-start.27 = (bf16[64,1024]{1,0:T(8,128)(2,1)S(1)}, bf16[64,1024]{1,0:T(8,128)(2,1)S(1)}, u32[]{:S(2)}, u32[]{:S(2)}) collective-permute-start(bf16[64,1024]{1,0:T(8,128)(2,1)S(1)} %grad_pre.4.refs_0_), channel_id=1, source_target_pairs={{0,32},{32,64},{64,96},{96,0},{1,33},{33,65},{65,97},{97,1},{2,34}... | collective-permute-start | bytes 393224 | tf_op jit(solution)/shard_map/ppermute | solution.py:330
  (28 other events, 300.3 us)

commit v2 on v1

--- a/solution.py
+++ b/solution.py
@@ -40,39 +40,52 @@
     return pl.BlockSpec(memory_space=VMEM)
 
 
-def split_matmul(me, rows4, lane, half, weight, transposed, size):
+def split_matmul(me, rows4, lane, half, weight, transposed, size, tile=512, keep=False, kept=False, away=False):
     peers, _, slot_rows, inner = rows4.shape
     halves = 2 if half is None else 1
     my_peers = peers * halves // 2
     first = 0 if half is None else half * my_peers
     count = my_peers * slot_rows
     quarter = count // (size * halves)
-    outer = weight.shape[0] if transposed else weight.shape[1]
-    tile = min(256, outer)
-
-    def body(me_ref, x_any, w_any, own_ref, *rest):
-        sends, (acc, x_ref, w_ref, x_sem, w_sem) = rest[:-5], rest[-5:]
+    if kept:
+        tiles = weight.shape
+        outer = tiles[0] * (tiles[1] if transposed else tiles[2])
+    else:
+        outer = weight.shape[0] if transposed else weight.shape[1]
+        tiles = (outer // tile, tile, inner) if transposed else (outer // tile, inner, tile)
+    tile = outer // tiles[0]
+
+    def body(me_ref, x_any, w_any, *rest):
+        own_ref, sends, rest = rest[0], rest[1:size], rest[size:]
+        if keep:
+            w_ref, rest = rest[0], rest[1:]
+        if kept:
+            w_ref = w_any
+        acc, x_ref, x_sem = rest[:3]
+        if not (keep or kept):
+            w_ref = rest[3]
+        w_sem = rest[-1]
+
+        def fetch(n):
+            cols = pl.ds(n * tile, tile)
+            source = w_any.at[cols, :] if transposed else w_any.at[:, cols]
+            return pltpu.make_async_copy(source, w_ref.at[n], w_sem.at[n])
+
         x_copy = pltpu.make_async_copy(x_any.at[pl.ds(first, my_peers), lane], x_ref, x_sem)
         x_copy.start()
-
-        def fetch(n):
-            cols = pl.ds(pl.multiple_of(n * tile, tile), tile)
-            source = w_any.at[cols, :] if transposed else w_any.at[:, cols]
-            return pltpu.make_async_copy(source, w_ref.at[n], w_sem.at[n])
-
-        for n in range(outer // tile):
-            fetch(n).start()
+        if not kept:
+            for n in range(tiles[0]):
+                fetch(n).start()
         x_copy.wait()
 
-        @pl.loop(0, outer // tile)
-        def _(n):
-            fetch(n).wait()
+        for n in range(tiles[0]):
+            if not kept:
+                fetch(n).wait()
             rows = x_ref[...].reshape(count, inner)
             dims = ((1,), (1,)) if transposed else ((1,), (0,))
-            acc[:, pl.ds(pl.multiple_of(n * tile, tile), tile)] = dot(rows, w_ref[n], dims)
+            acc[:, n * tile : (n + 1) * tile] = dot(rows, w_ref[n], dims)
 
         mine = me_ref[0]
-
         for h in range(halves):
             to = pl.ds(h * quarter, quarter)
 
@@ -86,20 +99,26 @@
 
     return pl.pallas_call(
         body,
-        in_specs=[pl.BlockSpec(memory_space=pltpu.SMEM)] + [pl.BlockSpec(memory_space=pl.ANY), pl.BlockSpec(memory_space=pltpu.HBM)],
-        out_specs=[whole()] * size,
-        out_shape=[jax.ShapeDtypeStruct((halves * quarter, outer), F32)]
-        + [jax.ShapeDtypeStruct((halves * quarter, outer), BF16)] * (size - 1),
+        in_specs=[
+            pl.BlockSpec(memory_space=pltpu.SMEM),
+            pl.BlockSpec(memory_space=pl.ANY),
+            whole() if kept else pl.BlockSpec(memory_space=pltpu.HBM),
+        ],
+        out_specs=[pl.BlockSpec((halves * quarter, outer), lambda: (0, 0)) if away else whole()]
+        + [whole()] * (size - 1 + (1 if keep else 0)),
+        out_shape=[(pltpu.HBM if away else jax.ShapeDtypeStruct)((halves * quarter, outer), F32)]
+        + [jax.ShapeDtypeStruct((halves * quarter, outer), BF16)] * (size - 1)
+        + ([VMEM(tiles, BF16)] if keep else []),
         scratch_shapes=[
             pltpu.VMEM((count, outer), F32),
             pltpu.VMEM((my_peers, slot_rows, inner), BF16),
-            pltpu.VMEM((outer // tile, tile, inner) if transposed else (outer // tile, inner, tile), BF16),
             pltpu.SemaphoreType.DMA,
-            pltpu.SemaphoreType.DMA((outer // tile,)),
-        ],
+        ]
+        + ([] if keep or kept else [pltpu.VMEM(tiles, BF16)])
+        + ([] if kept else [pltpu.SemaphoreType.DMA((tiles[0],))]),
         compiler_params=params(20),
         name="split_matmul",
-    )(me, rows4, weight)
+    )(me, rows4, near(weight) if kept else weight)
 
 
 def assemble(me, parts, out_ref, size):
@@ -115,7 +134,7 @@
 def decode(me, pieces, w_dec, peers, slot_rows, lanes, lane, size):
     count = peers * slot_rows
     inner, outer = w_dec.shape
-    tile = 512
+    tile = 1024
 
     def body(me_ref, *refs):
         parts, w_ref, out_ref, act_ref = refs[:-3], refs[-3], refs[-2], refs[-1]
@@ -142,31 +161,33 @@
             pltpu.HBM((peers, lanes, slot_rows, outer), BF16),
             pltpu.HBM((count, inner), BF16),
         ],
-        compiler_params=params(),
+        compiler_params=params(24),
         name="decode",
     )(me, *pieces, w_dec)
 
 
-def residual_rows(selector, returned, lane, x, bias_dec, scale, target, target_lane):
+def residual_rows(selector, returned, lane, blocks, chunk, bias_dec, scale, target, target_lane):
     peers, _, slot_rows, cols = returned.shape
     count = peers * slot_rows
     home = selector.shape[1]
-    tile = 512
+    block_count, rows_block, _ = blocks.shape
+    tile = 1024
 
     def body(sel_ref, got_ref, x_ref, b_ref, *rest):
         out_ref = rest[-1]
         sel = sel_ref[...]
         rebuilt = dot(sel, got_ref[...].reshape(count, tile), ((0,), (0,))) + b_ref[...]
-        residual = ((rebuilt - x_ref[...].astype(F32)) * scale).astype(BF16)
+        rows = x_ref[...].reshape(home, tile)
+        residual = ((rebuilt - rows.astype(F32)) * scale).astype(BF16)
         out_ref[...] = dot(sel, residual).astype(BF16).reshape(peers, 1, slot_rows, tile)
 
     in_specs = [
         whole(),
         pl.BlockSpec((peers, 1, slot_rows, tile), lambda n: (0, lane, 0, n)),
-        pl.BlockSpec((home, tile), lambda n: (0, n)),
+        pl.BlockSpec((block_count, rows_block // CHUNKS, tile), lambda n: (0, chunk, n)),
         pl.BlockSpec((1, tile), lambda n: (0, n)),
     ]
-    operands = [selector, returned, x, bias_dec]
+    operands = [selector, returned, blocks, bias_dec]
     aliases = {}
     lanes = 1
     if target is not None:
@@ -181,7 +202,7 @@
         out_specs=pl.BlockSpec((peers, 1, slot_rows, tile), lambda n: (0, target_lane, 0, n)),
         out_shape=pltpu.HBM((peers, lanes, slot_rows, cols), BF16),
         input_output_aliases=aliases,
-        compiler_params=params(),
+        compiler_params=params(24),
         name="residual_rows",
     )(*operands)
 
@@ -193,8 +214,8 @@
     else:
         count, wide = left.shape[0] * left.shape[2], left.shape[3]
     out_cols = right[0].shape[-1]
-    tile = 512
     last = base is not None
+    tile = 512 if last and inside else 1024
 
     def body(me_ref, left_ref, *refs):
         right_refs = refs[: len(right)]
@@ -215,8 +236,7 @@
         total = dot(lhs, rhs, ((0,), (0,)))
         if last:
             base_ref = refs[len(right)]
-            more = base_ref[:, here] if inside else base_ref[...]
-            out_ref[...] = (total + more).astype(BF16)
+            out_ref[...] = (total + base_ref[:, here]).astype(BF16)
         elif inside:
             out_ref[:, here] = total
         else:
@@ -239,8 +259,8 @@
         )
     operands += right
     if last:
-        operands.append(near(base) if inside else base)
-        in_specs.append(whole() if inside else column_block)
+        operands.append(near(base))
+        in_specs.append(whole())
     if last:
         out_shape = jax.ShapeDtypeStruct((wide, out_cols), BF16)
     else:
@@ -252,14 +272,68 @@
         out_specs=whole() if inside and not last else column_block,
         out_shape=out_shape,
         scratch_shapes=[pltpu.VMEM((count, out_cols), BF16)] if pieces else [],
-        compiler_params=params(24),
+        compiler_params=params(22 if last else 30),
         name="outer_sum",
     )(*operands)
 
 
-def dispatch(selector, x, peers):
-    out = dot(selector, x).astype(BF16)
-    return out.reshape(peers, 1, out.shape[0] // peers, out.shape[1])
+def encoder_sum(me, left, pieces, base, size):
+    peers, _, slot_rows, wide = left.shape
+    count = peers * slot_rows
+    cols = pieces[0].shape[1]
+    tile = 512
+
+    def body(me_ref, left_ref, *refs):
+        rows_ref = refs[-1]
+        step = pl.program_id(0)
+        here = pl.ds(pl.multiple_of(step * tile, tile), tile)
+
+        @pl.when(step == 0)
+        def _():
+            assemble(me_ref[0], refs[: len(pieces)], rows_ref, size)
+
+        lhs = left_ref[...].reshape(count, tile)
+        total = dot(lhs, rows_ref[...], ((0,), (0,)))
+        refs[-2][...] = (total + refs[-3][here, :]).astype(BF16)
+
+    return pl.pallas_call(
+        body,
+        grid=(wide // tile,),
+        in_specs=[
+            pl.BlockSpec(memory_space=pltpu.SMEM),
+            pl.BlockSpec((peers, 1, slot_rows, tile), lambda n: (0, 0, 0, n)),
+        ]
+        + [whole()] * (len(pieces) + 1),
+        out_specs=pl.BlockSpec((tile, cols), lambda n: (n, 0)),
+        out_shape=jax.ShapeDtypeStruct((wide, cols), BF16),
+        scratch_shapes=[pltpu.VMEM((count, cols), BF16)],
+        compiler_params=params(20),
+        name="encoder_sum",
+    )(me, left, *pieces, near(base))
+
+
+def dispatch(selector, blocks, chunk, peers):
+    count, home = selector.shape
+    block_count, rows_block, cols = blocks.shape
+    sub = rows_block // CHUNKS
+    tile = 1024
+
+    def body(sel_ref, x_ref, out_ref):
+        out = dot(sel_ref[...], x_ref[...].reshape(home, tile)).astype(BF16)
+        out_ref[...] = out.reshape(out_ref.shape)
+
+    return pl.pallas_call(
+        body,
+        grid=(cols // tile,),
+        in_specs=[
+            whole(),
+            pl.BlockSpec((block_count, sub, tile), lambda n: (0, chunk, n)),
+        ],
+        out_specs=pl.BlockSpec((peers, 1, count // peers, tile), lambda n: (0, 0, 0, n)),
+        out_shape=pltpu.HBM((peers, 1, count // peers, cols), BF16),
+        compiler_params=params(),
+        name="dispatch",
+    )(selector, blocks)
 
 
 def exchange(rows4):
@@ -356,48 +430,59 @@
         slot_row[:, None] == jnp.arange(block_count * sub, dtype=jnp.int32)[None, :]
     ).astype(BF16)
 
-    blocks = acts.reshape(block_count, CHUNKS, sub, cols)
-    x_a = blocks[:, 0].reshape(block_count * sub, cols)
-    x_b = blocks[:, 1].reshape(block_count * sub, cols)
+    blocks = acts.reshape(block_count, rows_block, cols)
     bias_enc = b_enc.astype(F32).reshape(1, -1)
     bias_dec = b_dec.astype(F32).reshape(1, cols)
     scale = 1.0 / rows_block
     w_enc = far(w_enc)
     w_dec = far(w_dec)
 
-    def share(rows4, lane, half, weight, transposed):
-        return split_matmul(me, rows4, lane, half, weight, transposed, size)
-
-
-    in_a = exchange(dispatch(selector, x_a, peers))
-    in_b = exchange(after(dispatch(selector, x_b, peers), in_a))
+    def share(rows4, lane, weight, transposed, away=False):
+        return split_matmul(me, rows4, lane, None, weight, transposed, size, away=away)
+
+    def first_half(rows4, weight, transposed):
+        *pieces, tiles = split_matmul(me, rows4, 0, 0, weight, transposed, size, keep=True)
+        return pieces, tiles
+
+    def second_half(rows4, tiles, transposed):
+        return split_matmul(me, rows4, 0, 1, tiles, transposed, size, kept=True)
+
+
+    in_a = exchange(dispatch(selector, blocks, 0, peers))
+    in_b = exchange(after(dispatch(selector, blocks, 1, peers), in_a))
     gates_a, own_a = [], []
     for h in range(2):
-        pieces = share(in_a, 0, h, w_enc, False)
+        if h == 0:
+            pieces, tiles = first_half(in_a, w_enc, False)
+        else:
+            pieces = second_half(in_a, tiles, False)
         pieces = swap_pieces(pieces, size)
         gate, act = activate(pieces, bias_enc)
         gates_a.append(gate)
         own_a.append(act)
     pieces_a = spread(own_a[0], size) + spread(own_a[1], size)
-    enc_b = share(in_b, 0, None, w_enc, False)
+    enc_b = share(in_b, 0, w_enc, False, True)
     enc_b = swap_pieces(enc_b, size)
     part_a, act_a = decode(me, pieces_a, w_dec, peers, slot_rows, 1, 0, size)
     back_a = exchange(part_a)
     gate_b, own_b = activate(enc_b, bias_enc)
     pieces_b = spread(own_b, size)
     part_b, act_b = decode(me, pieces_b, w_dec, peers, slot_rows, 2, 0, size)
-    mixed = residual_rows(selector, back_a, 0, x_a, bias_dec, scale, part_b, 1)
+    mixed = residual_rows(selector, back_a, 0, blocks, 0, bias_dec, scale, part_b, 1)
     mixed = far(exchange(mixed))
-    resid_b = residual_rows(selector, mixed, 0, x_b, bias_dec, scale, None, 0)
+    resid_b = residual_rows(selector, mixed, 0, blocks, 1, bias_dec, scale, None, 0)
     last = exchange(resid_b)
-    back = share(mixed, 1, None, w_dec, True)
+    back = share(mixed, 1, w_dec, True)
     back = swap_pieces(back, size)
     dec_sum = outer_sum(me, act_a, None, [mixed], 1, None, size, False)
     gp_a = grad_pre(back, gates_a, 0)
     pre_a = spread(gp_a, size)
     backs = []
     for h in range(2):
-        pieces = share(last, 0, h, w_dec, True)
+        if h == 0:
+            pieces, tiles = first_half(last, w_dec, True)
+        else:
+            pieces = second_half(last, tiles, True)
         backs.append(swap_pieces(pieces, size))
     enc_sum = outer_sum(me, in_a, 0, pre_a, None, None, size, True)
     half = gate_b.shape[0] // 2
@@ -409,7 +494,7 @@
         gp_b = grad_pre(pieces, [gate_b], h * half)
         pre_b += spread(gp_b, size)
     grad_dec = outer_sum(me, act_b, None, [last], 0, dec_sum, size, False)
-    grad_enc = outer_sum(me, in_b, 0, pre_b, None, enc_sum, size, True)
+    grad_enc = encoder_sum(me, in_b, pre_b, enc_sum, size)
     return grad_enc, grad_dec
 
 

time: 292 us -> 285 us (0.976)
  Pallas kernels: 67.5 us -> 61.7 us
  waiting for transfers between devices: 80.6 us -> 85.8 us
  matrix products: 5.19 us -> 0 us
    pallas_call x4 -> x3, Pallas kernels: 20.3 us -> 12.5 us  [outer_sum(): pl.pallas_call(body, grid=(out_cols // tile,), in_specs=in_specs, out_spe...]
    pallas_call x6 -> x9, Pallas kernels: 24.3 us -> 29.5 us  [the longest x6 20 us: split_matmul(): pl.pallas_call(body, in_specs=[pl.BlockSpec(memory_space=pltpu.SMEM), pl....]
    dot_general x2 -> x0, matrix products: 5.19 us -> none  [dot(): return lax.dot_general(a, b, (dims, ((), ())), preferred_element_type=F32)]
    ppermute x18, waiting for transfers between devices: 29 us -> 32.2 us  [swap_pieces(): out.append(lax.ppermute(pieces[shift], 'dp', ring(size, shift)))]
    unnamed x25 -> x27, local copies, waits for them, and re-layouts: 4.28 us -> 6.44 us
  transfers between devices with their start and end apart: 40 -> 40, of which waited for: 18 -> 18; matrix products, arithmetic and copies ran while one was open for 1% -> 0% of each run, Pallas kernels for 19% -> 17%
where the time goes in v2:
time: 285 us; the launch traced here: 281 us
  waiting for transfers between devices  85.8 us (30%)
  starting transfers between devices  66.3 us (23%)
  Pallas kernels  61.7 us (22%)
  blocking collectives  58.5 us (21%)
  local copies, waits for them, and re-layouts  6.62 us (2%)
    all_to_all x1, blocking collectives, exchange(): got = lax.all_to_all(flat, 'dict', split_axis=0, concat_axis=0, tiled=True)  58.5 us
    ppermute x18, waiting for transfers between devices, swap_pieces(): out.append(lax.ppermute(pieces[shift], 'dp', ring(size, shift)))  32.2 us
    all_to_all x4, waiting for transfers between devices, exchange(): got = lax.all_to_all(flat, 'dict', split_axis=0, concat_axis=0, tiled=True)  31.4 us
    all_to_all x4, starting transfers between devices, exchange(): got = lax.all_to_all(flat, 'dict', split_axis=0, concat_axis=0, tiled=True)  27.2 us
    ppermute x18, waiting for transfers between devices, spread(): out.append(lax.ppermute(own, 'dp', ring(size, shift)))  22.3 us
    ppermute x18, starting transfers between devices, swap_pieces(): out.append(lax.ppermute(pieces[shift], 'dp', ring(size, shift)))  20 us
    pallas_call x6, Pallas kernels, split_matmul(): pl.pallas_call(body, in_specs=[pl.BlockSpec(memory_space=pltpu.SMEM), pl....  20 us
    ppermute x18, starting transfers between devices, spread(): out.append(lax.ppermute(own, 'dp', ring(size, shift)))  19.1 us
  transfers between devices with their start and end apart: 40, of which 18 were waited for; matrix products, arithmetic and copies ran while one was open for 0% of the time, Pallas kernels for 17%

profile of v2, /device:TPU:1, one launch (start us, length us, event | category | flops | bytes accessed | tf_op | source)
XLA Modules:
  0.0 280.6 jit_solution(13390853350280147749)
XLA Ops:
  5.3 9.4 %all-to-all-start = ((bf16[32,16,2048]{2,1,0:T(8,128)(2,1)}), bf16[32,16,2048]{2,1,0:T(8,128)(2,1)S(1)}, u32[]{:S(2)}, u32[]{:S(2)}) async-start(bf16[32,16,2048]{2,1,0:T(8,128)(2,1)} %bitcast.36), calls=%async_computation | async-start | bytes 4194304 | tf_op jit(solution)/shard_map/all_to_all | solution.py:342
  16.7 26.4 %all-to-all-done = bf16[32,16,2048]{2,1,0:T(8,128)(2,1)S(1)} async-done(((bf16[32,16,2048]{2,1,0:T(8,128)(2,1)}), bf16[32,16,2048]{2,1,0:T(8,128)(2,1)S(1)}, u32[]{:S(2)}, u32[]{:S(2)}) %all-to-all-start) | async-done | bytes 2097184 | tf_op jit(solution)/shard_map/all_to_all | solution.py:342
  43.1 5.2 %all-to-all-start.1 = ((bf16[32,16,2048]{2,1,0:T(8,128)(2,1)}), bf16[32,16,2048]{2,1,0:T(8,128)(2,1)}, u32[]{:S(2)}, u32[]{:S(2)}) async-start(bf16[32,16,2048]{2,1,0:T(8,128)(2,1)} %bitcast.35), calls=%async_computation.1 | async-start | bytes 4194304 | tf_op jit(solution)/shard_map/all_to_all | solution.py:342
  76.2 3.2 %collective-permute-done.9.refs_5_ = bf16[64,1024]{1,0:T(8,128)(2,1)S(1)} collective-permute-done((bf16[64,1024]{1,0:T(8,128)(2,1)S(1)}, bf16[64,1024]{1,0:T(8,128)(2,1)S(1)}, u32[]{:S(2)}, u32[]{:S(2)}) %collective-permute-start.9) | collective-permute-done | bytes 131104 | tf_op jit(solution)/shard_map/ppermute | solution.py:404
  79.4 5.2 %decode.2 = (bf16[32,1,16,2048]{3,2,1,0:T(8,128)(2,1)}, bf16[512,1024]{1,0:T(8,128)(2,1)}) custom-call(s32[1]{0:T(128)} %bitcast.me_ref, bf16[64,1024]{1,0:T(8,128)(2,1)S(1)} %get-tuple-element.45.refs_0_, bf16[64,1024]{1,0:T(8,128)(2,1)S(1)} %collective-permute-done.3.refs_1_, bf16[64,1024]{1,0:T(8,128)(2,1)S(1)} %collective-permute-done.4.refs_2_, ...), custom_call_target="tpu_custom_call" | custom-call | tf_op jit(solution)/shard_map/decode/pallas_call | solution.py:150
  84.6 8.7 %all-to-all-start.2 = ((bf16[32,16,2048]{2,1,0:T(8,128)(2,1)}), bf16[32,16,2048]{2,1,0:T(8,128)(2,1)S(1)}, u32[]{:S(2)}, u32[]{:S(2)}) async-start(bf16[32,16,2048]{2,1,0:T(8,128)(2,1)} %bitcast.37), calls=%async_computation.2 | async-start | bytes 4194304 | tf_op jit(solution)/shard_map/all_to_all | solution.py:342
  93.4 5.7 %split_matmul.8 = (f32[128,1024]{1,0:T(8,128)}, bf16[128,1024]{1,0:T(8,128)(2,1)S(1)}, bf16[128,1024]{1,0:T(8,128)(2,1)S(1)}, bf16[128,1024]{1,0:T(8,128)(2,1)S(1)}) custom-call(s32[1]{0:T(128)} %bitcast.me_ref, bf16[32,1,16,2048]{3,2,1,0:T(8,128)(2,1)} %bitcast.5.x_any.left_ref, bf16[2048,1024]{1,0:T(8,128)(2,1)} %w_any.5), custom_call_target="tpu_custom_call" | custom-call | tf_op jit(solution)/shard_map/split_matmul/pallas_call | solution.py:100
  101.8 6.3 %collective-permute-done.12.refs_1_ = bf16[128,1024]{1,0:T(8,128)(2,1)S(1)} collective-permute-done((bf16[128,1024]{1,0:T(8,128)(2,1)S(1)}, bf16[128,1024]{1,0:T(8,128)(2,1)S(1)}, u32[]{:S(2)}, u32[]{:S(2)}) %collective-permute-start.12) | collective-permute-done | bytes 262176 | tf_op jit(solution)/shard_map/ppermute | solution.py:349
  108.2 5.2 %collective-permute-done.13.refs_2_ = bf16[128,1024]{1,0:T(8,128)(2,1)S(1)} collective-permute-done((bf16[128,1024]{1,0:T(8,128)(2,1)S(1)}, bf16[128,1024]{1,0:T(8,128)(2,1)S(1)}, u32[]{:S(2)}, u32[]{:S(2)}) %collective-permute-start.13) | collective-permute-done | bytes 262176 | tf_op jit(solution)/shard_map/ppermute | solution.py:349
  119.2 6.0 %collective-permute-done.17.refs_3_ = bf16[128,1024]{1,0:T(8,128)(2,1)S(1)} collective-permute-done((bf16[128,1024]{1,0:T(8,128)(2,1)S(1)}, bf16[128,1024]{1,0:T(8,128)(2,1)S(1)}, u32[]{:S(2)}, u32[]{:S(2)}) %collective-permute-start.17) | collective-permute-done | bytes 262176 | tf_op jit(solution)/shard_map/ppermute | solution.py:404
  127.1 6.3 %collective-permute-done.15.refs_1_ = bf16[128,1024]{1,0:T(8,128)(2,1)S(1)} collective-permute-done((bf16[128,1024]{1,0:T(8,128)(2,1)S(1)}, bf16[128,1024]{1,0:T(8,128)(2,1)S(1)}, u32[]{:S(2)}, u32[]{:S(2)}) %collective-permute-start.15) | collective-permute-done | bytes 262176 | tf_op jit(solution)/shard_map/ppermute | solution.py:404
  133.4 5.6 %decode.3 = (bf16[32,2,16,2048]{3,2,1,0:T(8,128)(2,1)}, bf16[512,1024]{1,0:T(8,128)(2,1)}) custom-call(s32[1]{0:T(128)} %bitcast.me_ref, bf16[128,1024]{1,0:T(8,128)(2,1)S(1)} %get-tuple-element.57.refs_0_, bf16[128,1024]{1,0:T(8,128)(2,1)S(1)} %collective-permute-done.15.refs_1_, bf16[128,1024]{1,0:T(8,128)(2,1)S(1)} %collective-permute-done.16.refs_2_, ...), custom_call_target="tpu_custom_call" | custom-call | tf_op jit(solution)/shard_map/decode/pallas_call | solution.py:150
  141.5 58.5 %all_to_all.25 = bf16[32,32,2048]{2,1,0:T(8,128)(2,1)} all-to-all(bf16[32,32,2048]{2,1,0:T(8,128)(2,1)} %bitcast.33), channel_id=1, replica_groups=mesh['dp'=4,'dict'=32] {'dict'}, dimensions={0} | all-to-all | bytes 8388608 | tf_op jit(solution)/shard_map/all_to_all | solution.py:342
  200.0 3.6 %residual_rows.3 = bf16[32,1,16,2048]{3,2,1,0:T(8,128)(2,1)} custom-call(bf16[512,128]{1,0:T(8,128)(2,1)S(1)} %fusion.sel_ref, bf16[32,2,16,2048]{3,2,1,0:T(8,128)(2,1)} %bitcast.30, bf16[16,16,2048]{2,1,0:T(8,128)(2,1)S(1)} %bitcast.23, f32[1,2048]{1,0:T(1,128)S(1)} %bitcast.26), custom_call_target="tpu_custom_call" | custom-call | tf_op jit(solution)/shard_map/residual_rows/pallas_call | solution.py:198
  203.6 3.9 %all-to-all-start.4 = ((bf16[32,16,2048]{2,1,0:T(8,128)(2,1)}), bf16[32,16,2048]{2,1,0:T(8,128)(2,1)S(1)}, u32[]{:S(2)}, u32[]{:S(2)}) async-start(bf16[32,16,2048]{2,1,0:T(8,128)(2,1)} %bitcast.34), calls=%async_computation.4 | async-start | bytes 4194304 | tf_op jit(solution)/shard_map/all_to_all | solution.py:342
  207.5 5.0 %split_matmul.10 = (f32[128,1024]{1,0:T(8,128)S(1)}, bf16[128,1024]{1,0:T(8,128)(2,1)S(1)}, bf16[128,1024]{1,0:T(8,128)(2,1)S(1)}, bf16[128,1024]{1,0:T(8,128)(2,1)S(1)}) custom-call(s32[1]{0:T(128)} %bitcast.me_ref, bf16[32,2,16,2048]{3,2,1,0:T(8,128)(2,1)} %bitcast.31, bf16[1024,2048]{1,0:T(8,128)(2,1)} %w_any.7), custom_call_target="tpu_custom_call" | custom-call | tf_op jit(solution)/shard_map/split_matmul/pallas_call | solution.py:100
  215.3 11.8 %collective-permute-done.18.refs_1_ = bf16[128,1024]{1,0:T(8,128)(2,1)S(1)} collective-permute-done((bf16[128,1024]{1,0:T(8,128)(2,1)S(1)}, bf16[128,1024]{1,0:T(8,128)(2,1)S(1)}, u32[]{:S(2)}, u32[]{:S(2)}) %collective-permute-start.18) | collective-permute-done | bytes 262176 | tf_op jit(solution)/shard_map/ppermute | solution.py:349
  231.0 4.9 %all-to-all-done.4 = bf16[32,16,2048]{2,1,0:T(8,128)(2,1)S(1)} async-done(((bf16[32,16,2048]{2,1,0:T(8,128)(2,1)}), bf16[32,16,2048]{2,1,0:T(8,128)(2,1)S(1)}, u32[]{:S(2)}, u32[]{:S(2)}) %all-to-all-start.4) | async-done | bytes 2097184 | tf_op jit(solution)/shard_map/all_to_all | solution.py:342
  235.9 3.2 %split_matmul.9 = (f32[64,1024]{1,0:T(8,128)S(1)}, bf16[64,1024]{1,0:T(8,128)(2,1)S(1)}, bf16[64,1024]{1,0:T(8,128)(2,1)S(1)}, bf16[64,1024]{1,0:T(8,128)(2,1)S(1)}, bf16[2,512,2048]{2,1,0:T(8,128)(2,1)S(1)}) custom-call(s32[1]{0:T(128)} %bitcast.me_ref, bf16[32,1,16,2048]{3,2,1,0:T(8,128)(2,1)S(1)} %bitcast.14, bf16[1024,2048]{1,0:T(8,128)(2,1)} %w_any.7), custom_call_target="tpu_custom_call" | custom-call | tf_op jit(solution)/shard_map/split_matmul/pallas_call | solution.py:100
  244.2 4.4 %collective-permute-done.30.refs_1_ = bf16[64,1024]{1,0:T(8,128)(2,1)S(1)} collective-permute-done((bf16[64,1024]{1,0:T(8,128)(2,1)S(1)}, bf16[64,1024]{1,0:T(8,128)(2,1)S(1)}, u32[]{:S(2)}, u32[]{:S(2)}) %collective-permute-start.30) | collective-permute-done | bytes 131104 | tf_op jit(solution)/shard_map/ppermute | solution.py:349
  261.2 6.0 %outer_sum.4.refs_1_ = f32[1024,2048]{1,0:T(8,128)} custom-call(s32[1]{0:T(128)} %bitcast.me_ref, bf16[512,1024]{1,0:T(8,128)(2,1)S(1)} %copy-done.7, bf16[32,2,16,2048]{3,2,1,0:T(8,128)(2,1)} %bitcast.32), custom_call_target="tpu_custom_call" | custom-call | tf_op jit(solution)/shard_map/outer_sum/pallas_call | solution.py:268
  267.3 3.4 %copy-done = f32[1024,2048]{1,0:T(8,128)S(1)} copy-done((f32[1024,2048]{1,0:T(8,128)S(1)}, f32[1024,2048]{1,0:T(8,128)}, u32[]{:S(2)}) %copy-start) | copy-done | bytes 8388632
  270.6 4.1 %outer_sum.5 = bf16[1024,2048]{1,0:T(8,128)(2,1)} custom-call(s32[1]{0:T(128)} %bitcast.me_ref, bf16[512,1024]{1,0:T(8,128)(2,1)S(1)} %copy-done.6, bf16[32,1,16,2048]{3,2,1,0:T(8,128)(2,1)S(1)} %bitcast.16, f32[1024,2048]{1,0:T(8,128)S(1)} %copy-done), custom_call_target="tpu_custom_call" | custom-call | tf_op jit(solution)/shard_map/outer_sum/pallas_call | solution.py:268
  274.7 5.8 %encoder_sum.1 = bf16[2048,1024]{1,0:T(8,128)(2,1)} custom-call(s32[1]{0:T(128)} %bitcast.me_ref, bf16[32,1,16,2048]{3,2,1,0:T(8,128)(2,1)} %bitcast.5.x_any.left_ref, bf16[64,1024]{1,0:T(8,128)(2,1)S(1)} %grad_pre.4.refs_0_, bf16[64,1024]{1,0:T(8,128)(2,1)S(1)} %collective-permute-done.27.refs_1_, bf16[64,1024]{1,0:T(8,128)(2,1)S(1)} %collective-permute-done.28.refs_2_, ...), custom_call_target="tpu_custom_call" | custom-call | tf_op jit(solution)/shard_map/encoder_sum/pallas_call | solution.py:299
  (119 shorter events, 71.8 us)
Async XLA Ops:
  5.3 37.8 %all-to-all-start = ((bf16[32,16,2048]{2,1,0:T(8,128)(2,1)}), bf16[32,16,2048]{2,1,0:T(8,128)(2,1)S(1)}, u32[]{:S(2)}, u32[]{:S(2)}) async-start(bf16[32,16,2048]{2,1,0:T(8,128)(2,1)} %bitcast.36), calls=%async_computation | async-start | bytes 4194304 | tf_op jit(solution)/shard_map/all_to_all | solution.py:342
  43.1 41.5 %all-to-all-start.1 = ((bf16[32,16,2048]{2,1,0:T(8,128)(2,1)}), bf16[32,16,2048]{2,1,0:T(8,128)(2,1)}, u32[]{:S(2)}, u32[]{:S(2)}) async-start(bf16[32,16,2048]{2,1,0:T(8,128)(2,1)} %bitcast.35), calls=%async_computation.1 | async-start | bytes 4194304 | tf_op jit(solution)/shard_map/all_to_all | solution.py:342
  52.9 8.7 %collective-permute-start.1 = (bf16[64,1024]{1,0:T(8,128)(2,1)S(1)}, bf16[64,1024]{1,0:T(8,128)(2,1)S(1)}, u32[]{:S(2)}, u32[]{:S(2)}) collective-permute-start(bf16[64,1024]{1,0:T(8,128)(2,1)S(1)} %get-tuple-element.43), channel_id=1, source_target_pairs={{0,64},{32,96},{64,0},{96,32},{1,65},{33,97},{65,1},{97,33},{2,66}... | collective-permute-start | bytes 393224 | tf_op jit(solution)/shard_map/ppermute | solution.py:349
  58.5 8.8 %collective-permute-start.7 = (bf16[64,1024]{1,0:T(8,128)(2,1)S(1)}, bf16[64,1024]{1,0:T(8,128)(2,1)S(1)}, u32[]{:S(2)}, u32[]{:S(2)}) collective-permute-start(bf16[64,1024]{1,0:T(8,128)(2,1)S(1)} %get-tuple-element.49), channel_id=1, source_target_pairs={{0,64},{32,96},{64,0},{96,32},{1,65},{33,97},{65,1},{97,33},{2,66}... | collective-permute-start | bytes 393224 | tf_op jit(solution)/shard_map/ppermute | solution.py:349
  62.4 8.6 %collective-permute-start.5 = (bf16[64,1024]{1,0:T(8,128)(2,1)S(1)}, bf16[64,1024]{1,0:T(8,128)(2,1)S(1)}, u32[]{:S(2)}, u32[]{:S(2)}) collective-permute-start(bf16[64,1024]{1,0:T(8,128)(2,1)S(1)} %get-tuple-element.45.refs_0_), channel_id=1, source_target_pairs={{0,96},{32,0},{64,32},{96,64},{1,97},{33,1},{65,33},{97,65},{2,98}... | collective-permute-start | bytes 393224 | tf_op jit(solution)/shard_map/ppermute | solution.py:404
  84.6 54.3 %all-to-all-start.2 = ((bf16[32,16,2048]{2,1,0:T(8,128)(2,1)}), bf16[32,16,2048]{2,1,0:T(8,128)(2,1)S(1)}, u32[]{:S(2)}, u32[]{:S(2)}) async-start(bf16[32,16,2048]{2,1,0:T(8,128)(2,1)} %bitcast.37), calls=%async_computation.2 | async-start | bytes 4194304 | tf_op jit(solution)/shard_map/all_to_all | solution.py:342
  99.0 9.2 %collective-permute-start.12 = (bf16[128,1024]{1,0:T(8,128)(2,1)S(1)}, bf16[128,1024]{1,0:T(8,128)(2,1)S(1)}, u32[]{:S(2)}, u32[]{:S(2)}) collective-permute-start(bf16[128,1024]{1,0:T(8,128)(2,1)S(1)} %get-tuple-element.54), channel_id=1, source_target_pairs={{0,32},{32,64},{64,96},{96,0},{1,33},{33,65},{65,97},{97,1},{2,34}... | collective-permute-start | bytes 786440 | tf_op jit(solution)/shard_map/ppermute | solution.py:349
  99.4 14.0 %collective-permute-start.13 = (bf16[128,1024]{1,0:T(8,128)(2,1)S(1)}, bf16[128,1024]{1,0:T(8,128)(2,1)S(1)}, u32[]{:S(2)}, u32[]{:S(2)}) collective-permute-start(bf16[128,1024]{1,0:T(8,128)(2,1)S(1)} %get-tuple-element.55), channel_id=1, source_target_pairs={{0,64},{32,96},{64,0},{96,32},{1,65},{33,97},{65,1},{97,33},{2,66}... | collective-permute-start | bytes 786440 | tf_op jit(solution)/shard_map/ppermute | solution.py:349
  101.5 12.4 %collective-permute-start.14 = (bf16[128,1024]{1,0:T(8,128)(2,1)S(1)}, bf16[128,1024]{1,0:T(8,128)(2,1)S(1)}, u32[]{:S(2)}, u32[]{:S(2)}) collective-permute-start(bf16[128,1024]{1,0:T(8,128)(2,1)S(1)} %get-tuple-element.56), channel_id=1, source_target_pairs={{0,96},{32,0},{64,32},{96,64},{1,97},{33,1},{65,33},{97,65},{2,98}... | collective-permute-start | bytes 786440 | tf_op jit(solution)/shard_map/ppermute | solution.py:349
  115.9 9.4 %collective-permute-start.17 = (bf16[128,1024]{1,0:T(8,128)(2,1)S(1)}, bf16[128,1024]{1,0:T(8,128)(2,1)S(1)}, u32[]{:S(2)}, u32[]{:S(2)}) collective-permute-start(bf16[128,1024]{1,0:T(8,128)(2,1)S(1)} %get-tuple-element.57.refs_0_), channel_id=1, source_target_pairs={{0,96},{32,0},{64,32},{96,64},{1,97},{33,1},{65,33},{97,65},{2,98}... | collective-permute-start | bytes 786440 | tf_op jit(solution)/shard_map/ppermute | solution.py:404
  118.6 14.8 %collective-permute-start.15 = (bf16[128,1024]{1,0:T(8,128)(2,1)S(1)}, bf16[128,1024]{1,0:T(8,128)(2,1)S(1)}, u32[]{:S(2)}, u32[]{:S(2)}) collective-permute-start(bf16[128,1024]{1,0:T(8,128)(2,1)S(1)} %get-tuple-element.57.refs_0_), channel_id=1, source_target_pairs={{0,32},{32,64},{64,96},{96,0},{1,33},{33,65},{65,97},{97,1},{2,34}... | collective-permute-start | bytes 786440 | tf_op jit(solution)/shard_map/ppermute | solution.py:404
  203.6 32.3 %all-to-all-start.4 = ((bf16[32,16,2048]{2,1,0:T(8,128)(2,1)}), bf16[32,16,2048]{2,1,0:T(8,128)(2,1)S(1)}, u32[]{:S(2)}, u32[]{:S(2)}) async-start(bf16[32,16,2048]{2,1,0:T(8,128)(2,1)} %bitcast.34), calls=%async_computation.4 | async-start | bytes 4194304 | tf_op jit(solution)/shard_map/all_to_all | solution.py:342
  212.5 14.5 %collective-permute-start.18 = (bf16[128,1024]{1,0:T(8,128)(2,1)S(1)}, bf16[128,1024]{1,0:T(8,128)(2,1)S(1)}, u32[]{:S(2)}, u32[]{:S(2)}) collective-permute-start(bf16[128,1024]{1,0:T(8,128)(2,1)S(1)} %get-tuple-element.61), channel_id=1, source_target_pairs={{0,32},{32,64},{64,96},{96,0},{1,33},{33,65},{65,97},{97,1},{2,34}... | collective-permute-start | bytes 786440 | tf_op jit(solution)/shard_map/ppermute | solution.py:349
  212.6 14.4 %collective-permute-start.19 = (bf16[128,1024]{1,0:T(8,128)(2,1)S(1)}, bf16[128,1024]{1,0:T(8,128)(2,1)S(1)}, u32[]{:S(2)}, u32[]{:S(2)}) collective-permute-start(bf16[128,1024]{1,0:T(8,128)(2,1)S(1)} %get-tuple-element.62), channel_id=1, source_target_pairs={{0,64},{32,96},{64,0},{96,32},{1,65},{33,97},{65,1},{97,33},{2,66}... | collective-permute-start | bytes 786440 | tf_op jit(solution)/shard_map/ppermute | solution.py:349
  214.4 13.0 %collective-permute-start.20 = (bf16[128,1024]{1,0:T(8,128)(2,1)S(1)}, bf16[128,1024]{1,0:T(8,128)(2,1)S(1)}, u32[]{:S(2)}, u32[]{:S(2)}) collective-permute-start(bf16[128,1024]{1,0:T(8,128)(2,1)S(1)} %get-tuple-element.63), channel_id=1, source_target_pairs={{0,96},{32,0},{64,32},{96,64},{1,97},{33,1},{65,33},{97,65},{2,98}... | collective-permute-start | bytes 786440 | tf_op jit(solution)/shard_map/ppermute | solution.py:349
  227.6 14.9 %collective-permute-start.23 = (bf16[128,1024]{1,0:T(8,128)(2,1)S(1)}, bf16[128,1024]{1,0:T(8,128)(2,1)S(1)}, u32[]{:S(2)}, u32[]{:S(2)}) collective-permute-start(bf16[128,1024]{1,0:T(8,128)(2,1)S(1)} %grad_pre.3.refs_0_), channel_id=1, source_target_pairs={{0,96},{32,0},{64,32},{96,64},{1,97},{33,1},{65,33},{97,65},{2,98}... | collective-permute-start | bytes 786440 | tf_op jit(solution)/shard_map/ppermute | solution.py:404
  230.3 22.3 %collective-permute-start.22 = (bf16[128,1024]{1,0:T(8,128)(2,1)S(1)}, bf16[128,1024]{1,0:T(8,128)(2,1)S(1)}, u32[]{:S(2)}, u32[]{:S(2)}) collective-permute-start(bf16[128,1024]{1,0:T(8,128)(2,1)S(1)} %grad_pre.3.refs_0_), channel_id=1, source_target_pairs={{0,64},{32,96},{64,0},{96,32},{1,65},{33,97},{65,1},{97,33},{2,66}... | collective-permute-start | bytes 786440 | tf_op jit(solution)/shard_map/ppermute | solution.py:404
  230.3 22.8 %collective-permute-start.21 = (bf16[128,1024]{1,0:T(8,128)(2,1)S(1)}, bf16[128,1024]{1,0:T(8,128)(2,1)S(1)}, u32[]{:S(2)}, u32[]{:S(2)}) collective-permute-start(bf16[128,1024]{1,0:T(8,128)(2,1)S(1)} %grad_pre.3.refs_0_), channel_id=1, source_target_pairs={{0,32},{32,64},{64,96},{96,0},{1,33},{33,65},{65,97},{97,1},{2,34}... | collective-permute-start | bytes 786440 | tf_op jit(solution)/shard_map/ppermute | solution.py:404
  240.7 8.9 %collective-permute-start.31 = (bf16[64,1024]{1,0:T(8,128)(2,1)S(1)}, bf16[64,1024]{1,0:T(8,128)(2,1)S(1)}, u32[]{:S(2)}, u32[]{:S(2)}) collective-permute-start(bf16[64,1024]{1,0:T(8,128)(2,1)S(1)} %get-tuple-element.74), channel_id=1, source_target_pairs={{0,64},{32,96},{64,0},{96,32},{1,65},{33,97},{65,1},{97,33},{2,66}... | collective-permute-start | bytes 393224 | tf_op jit(solution)/shard_map/ppermute | solution.py:349
  255.5 19.2 %collective-permute-start.34 = (bf16[64,1024]{1,0:T(8,128)(2,1)S(1)}, bf16[64,1024]{1,0:T(8,128)(2,1)S(1)}, u32[]{:S(2)}, u32[]{:S(2)}) collective-permute-start(bf16[64,1024]{1,0:T(8,128)(2,1)S(1)} %grad_pre.5.refs_4_), channel_id=1, source_target_pairs={{0,64},{32,96},{64,0},{96,32},{1,65},{33,97},{65,1},{97,33},{2,66}... | collective-permute-start | bytes 393224 | tf_op jit(solution)/shard_map/ppermute | solution.py:404
  256.5 18.3 %collective-permute-start.33 = (bf16[64,1024]{1,0:T(8,128)(2,1)S(1)}, bf16[64,1024]{1,0:T(8,128)(2,1)S(1)}, u32[]{:S(2)}, u32[]{:S(2)}) collective-permute-start(bf16[64,1024]{1,0:T(8,128)(2,1)S(1)} %grad_pre.5.refs_4_), channel_id=1, source_target_pairs={{0,32},{32,64},{64,96},{96,0},{1,33},{33,65},{65,97},{97,1},{2,34}... | collective-permute-start | bytes 393224 | tf_op jit(solution)/shard_map/ppermute | solution.py:404
  257.3 17.4 %collective-permute-start.29 = (bf16[64,1024]{1,0:T(8,128)(2,1)S(1)}, bf16[64,1024]{1,0:T(8,128)(2,1)S(1)}, u32[]{:S(2)}, u32[]{:S(2)}) collective-permute-start(bf16[64,1024]{1,0:T(8,128)(2,1)S(1)} %grad_pre.4.refs_0_), channel_id=1, source_target_pairs={{0,96},{32,0},{64,32},{96,64},{1,97},{33,1},{65,33},{97,65},{2,98}... | collective-permute-start | bytes 393224 | tf_op jit(solution)/shard_map/ppermute | solution.py:404
  260.4 14.3 %collective-permute-start.28 = (bf16[64,1024]{1,0:T(8,128)(2,1)S(1)}, bf16[64,1024]{1,0:T(8,128)(2,1)S(1)}, u32[]{:S(2)}, u32[]{:S(2)}) collective-permute-start(bf16[64,1024]{1,0:T(8,128)(2,1)S(1)} %grad_pre.4.refs_0_), channel_id=1, source_target_pairs={{0,64},{32,96},{64,0},{96,32},{1,65},{33,97},{65,1},{97,33},{2,66}... | collective-permute-start | bytes 393224 | tf_op jit(solution)/shard_map/ppermute | solution.py:404
  260.5 14.3 %collective-permute-start.27 = (bf16[64,1024]{1,0:T(8,128)(2,1)S(1)}, bf16[64,1024]{1,0:T(8,128)(2,1)S(1)}, u32[]{:S(2)}, u32[]{:S(2)}) collective-permute-start(bf16[64,1024]{1,0:T(8,128)(2,1)S(1)} %grad_pre.4.refs_0_), channel_id=1, source_target_pairs={{0,32},{32,64},{64,96},{96,0},{1,33},{33,65},{65,97},{97,1},{2,34}... | collective-permute-start | bytes 393224 | tf_op jit(solution)/shard_map/ppermute | solution.py:404
  (29 other events, 265.0 us)

commit v3 on v2

--- a/solution.py
+++ b/solution.py
@@ -207,7 +207,7 @@
     )(*operands)
 
 
-def outer_sum(me, left, left_lane, right, right_lane, base, size, inside):
+def outer_sum(me, left, left_lane, right, right_lane, base, size, inside, carry=None):
     pieces = right_lane is None
     if left_lane is None:
         count, wide = left.shape
@@ -219,12 +219,15 @@
 
     def body(me_ref, left_ref, *refs):
         right_refs = refs[: len(right)]
-        out_ref = refs[len(right) + (1 if last else 0)]
+        out_ref = refs[len(right) + (1 if last or carry is not None else 0)]
         step = pl.program_id(0)
+        if carry is not None:
+            copy = pltpu.make_async_copy(refs[len(right)], refs[len(right) + 2], refs[-1])
+            copy.start()
         here = pl.ds(pl.multiple_of(step * tile, tile), tile)
         lhs = left_ref[...].reshape(count, wide)
         if pieces:
-            rows_ref = refs[-1]
+            rows_ref = refs[-1 if carry is None else -2]
 
             @pl.when(step == 0)
             def _():
@@ -241,6 +244,8 @@
             out_ref[:, here] = total
         else:
             out_ref[...] = total
+        if carry is not None:
+            copy.wait()
 
     column_block = pl.BlockSpec((wide, tile), lambda n: (0, n))
     in_specs = [pl.BlockSpec(memory_space=pltpu.SMEM)]
@@ -265,13 +270,22 @@
         out_shape = jax.ShapeDtypeStruct((wide, out_cols), BF16)
     else:
         out_shape = (VMEM if inside else pltpu.HBM)((wide, out_cols), F32)
+    out_specs = whole() if inside and not last else column_block
+    scratch = [pltpu.VMEM((count, out_cols), BF16)] if pieces else []
+    if carry is not None:
+        assert out_cols == tile
+        operands.append(carry)
+        in_specs.append(pl.BlockSpec(memory_space=pl.ANY))
+        out_shape = [out_shape, VMEM(carry.shape, carry.dtype)]
+        out_specs = [out_specs, whole()]
+        scratch.append(pltpu.SemaphoreType.DMA)
     return pl.pallas_call(
         body,
         grid=(out_cols // tile,),
         in_specs=in_specs,
-        out_specs=whole() if inside and not last else column_block,
+        out_specs=out_specs,
         out_shape=out_shape,
-        scratch_shapes=[pltpu.VMEM((count, out_cols), BF16)] if pieces else [],
+        scratch_shapes=scratch,
         compiler_params=params(22 if last else 30),
         name="outer_sum",
     )(*operands)
@@ -292,7 +306,7 @@
         def _():
             assemble(me_ref[0], refs[: len(pieces)], rows_ref, size)
 
-        lhs = left_ref[...].reshape(count, tile)
+        lhs = left_ref[:, 0, :, here].reshape(count, tile)
         total = dot(lhs, rows_ref[...], ((0,), (0,)))
         refs[-2][...] = (total + refs[-3][here, :]).astype(BF16)
 
@@ -301,7 +315,7 @@
         grid=(wide // tile,),
         in_specs=[
             pl.BlockSpec(memory_space=pltpu.SMEM),
-            pl.BlockSpec((peers, 1, slot_rows, tile), lambda n: (0, 0, 0, n)),
+            whole(),
         ]
         + [whole()] * (len(pieces) + 1),
         out_specs=pl.BlockSpec((tile, cols), lambda n: (n, 0)),
@@ -309,7 +323,7 @@
         scratch_shapes=[pltpu.VMEM((count, cols), BF16)],
         compiler_params=params(20),
         name="encoder_sum",
-    )(me, left, *pieces, near(base))
+    )(me, near(left), *pieces, near(base))
 
 
 def dispatch(selector, blocks, chunk, peers):
@@ -448,8 +462,8 @@
         return split_matmul(me, rows4, 0, 1, tiles, transposed, size, kept=True)
 
 
-    in_a = exchange(dispatch(selector, blocks, 0, peers))
-    in_b = exchange(after(dispatch(selector, blocks, 1, peers), in_a))
+    in_a = exchange(dispatch(selector, far(blocks), 0, peers))
+    in_b = exchange(after(dispatch(selector, far(blocks), 1, peers), in_a))
     gates_a, own_a = [], []
     for h in range(2):
         if h == 0:
@@ -475,6 +489,7 @@
     back = share(mixed, 1, w_dec, True)
     back = swap_pieces(back, size)
     dec_sum = outer_sum(me, act_a, None, [mixed], 1, None, size, False)
+    back[0] = after(back[0], dec_sum)
     gp_a = grad_pre(back, gates_a, 0)
     pre_a = spread(gp_a, size)
     backs = []
@@ -484,7 +499,7 @@
         else:
             pieces = second_half(last, tiles, True)
         backs.append(swap_pieces(pieces, size))
-    enc_sum = outer_sum(me, in_a, 0, pre_a, None, None, size, True)
+    enc_sum, in_b = outer_sum(me, in_a, 0, pre_a, None, None, size, True, in_b)
     half = gate_b.shape[0] // 2
     pre_b = []
     for h in range(2):

time: 285 us -> 277 us (0.972)
  local copies, waits for them, and re-layouts: 6.62 us -> 2.03 us
    ppermute x18, waiting for transfers between devices: 32.2 us -> 26.3 us  [swap_pieces(): out.append(lax.ppermute(pieces[shift], 'dp', ring(size, shift)))]
    unnamed x27, local copies, waits for them, and re-layouts: 6.44 us -> 1.86 us
    ppermute x18, waiting for transfers between devices: 22.3 us -> 26.5 us  [spread(): out.append(lax.ppermute(own, 'dp', ring(size, shift)))]
  transfers between devices with their start and end apart: 40 -> 40, of which waited for: 18 -> 22; matrix products, arithmetic and copies ran while one was open for 0% -> 0% of each run, Pallas kernels for 17% -> 18%
where the time goes in v3:
time: 277 us; the launch traced here: 274 us
  waiting for transfers between devices  83.2 us (30%)
  starting transfers between devices  66.6 us (24%)
  Pallas kernels  62.2 us (22%)
  blocking collectives  58.5 us (21%)
    all_to_all x1, blocking collectives, exchange(): got = lax.all_to_all(flat, 'dict', split_axis=0, concat_axis=0, tiled=True)  58.5 us
    all_to_all x4, waiting for transfers between devices, exchange(): got = lax.all_to_all(flat, 'dict', split_axis=0, concat_axis=0, tiled=True)  30.4 us
    all_to_all x4, starting transfers between devices, exchange(): got = lax.all_to_all(flat, 'dict', split_axis=0, concat_axis=0, tiled=True)  27.2 us
    ppermute x18, waiting for transfers between devices, spread(): out.append(lax.ppermute(own, 'dp', ring(size, shift)))  26.5 us
    ppermute x18, waiting for transfers between devices, swap_pieces(): out.append(lax.ppermute(pieces[shift], 'dp', ring(size, shift)))  26.3 us
    ppermute x18, starting transfers between devices, swap_pieces(): out.append(lax.ppermute(pieces[shift], 'dp', ring(size, shift)))  20.4 us
    pallas_call x6, Pallas kernels, split_matmul(): pl.pallas_call(body, in_specs=[pl.BlockSpec(memory_space=pltpu.SMEM), pl....  20.2 us
    ppermute x18, starting transfers between devices, spread(): out.append(lax.ppermute(own, 'dp', ring(size, shift)))  18.9 us
  transfers between devices with their start and end apart: 40, of which 22 were waited for; matrix products, arithmetic and copies ran while one was open for 0% of the time, Pallas kernels for 18%

profile of v3, /device:TPU:1, one launch (start us, length us, event | category | flops | bytes accessed | tf_op | source)
XLA Modules:
  0.0 274.1 jit_solution(7614008818266371082)
XLA Ops:
  5.0 9.4 %all-to-all-start = ((bf16[32,16,2048]{2,1,0:T(8,128)(2,1)}), bf16[32,16,2048]{2,1,0:T(8,128)(2,1)S(1)}, u32[]{:S(2)}, u32[]{:S(2)}) async-start(bf16[32,16,2048]{2,1,0:T(8,128)(2,1)} %bitcast.38), calls=%async_computation | async-start | bytes 4194304 | tf_op jit(solution)/shard_map/all_to_all | solution.py:356
  17.3 25.5 %all-to-all-done = bf16[32,16,2048]{2,1,0:T(8,128)(2,1)S(1)} async-done(((bf16[32,16,2048]{2,1,0:T(8,128)(2,1)}), bf16[32,16,2048]{2,1,0:T(8,128)(2,1)S(1)}, u32[]{:S(2)}, u32[]{:S(2)}) %all-to-all-start) | async-done | bytes 2097184 | tf_op jit(solution)/shard_map/all_to_all | solution.py:356
  42.8 5.2 %all-to-all-start.2 = ((bf16[32,16,2048]{2,1,0:T(8,128)(2,1)}), bf16[32,16,2048]{2,1,0:T(8,128)(2,1)}, u32[]{:S(2)}, u32[]{:S(2)}) async-start(bf16[32,16,2048]{2,1,0:T(8,128)(2,1)} %bitcast.37), calls=%async_computation.2 | async-start | bytes 4194304 | tf_op jit(solution)/shard_map/all_to_all | solution.py:356
  75.9 3.2 %collective-permute-done.9.refs_5_ = bf16[64,1024]{1,0:T(8,128)(2,1)S(1)} collective-permute-done((bf16[64,1024]{1,0:T(8,128)(2,1)S(1)}, bf16[64,1024]{1,0:T(8,128)(2,1)S(1)}, u32[]{:S(2)}, u32[]{:S(2)}) %collective-permute-start.9) | collective-permute-done | bytes 131104 | tf_op jit(solution)/shard_map/ppermute | solution.py:418
  79.1 5.2 %decode.2 = (bf16[32,1,16,2048]{3,2,1,0:T(8,128)(2,1)}, bf16[512,1024]{1,0:T(8,128)(2,1)}) custom-call(s32[1]{0:T(128)} %bitcast.me_ref, bf16[64,1024]{1,0:T(8,128)(2,1)S(1)} %get-tuple-element.47.refs_0_, bf16[64,1024]{1,0:T(8,128)(2,1)S(1)} %collective-permute-done.3.refs_1_, bf16[64,1024]{1,0:T(8,128)(2,1)S(1)} %collective-permute-done.4.refs_2_, ...), custom_call_target="tpu_custom_call" | custom-call | tf_op jit(solution)/shard_map/decode/pallas_call | solution.py:150
  84.3 8.7 %all-to-all-start.1 = ((bf16[32,16,2048]{2,1,0:T(8,128)(2,1)}), bf16[32,16,2048]{2,1,0:T(8,128)(2,1)S(1)}, u32[]{:S(2)}, u32[]{:S(2)}) async-start(bf16[32,16,2048]{2,1,0:T(8,128)(2,1)} %bitcast.39), calls=%async_computation.1 | async-start | bytes 4194304 | tf_op jit(solution)/shard_map/all_to_all | solution.py:356
  93.1 5.7 %split_matmul.8 = (f32[128,1024]{1,0:T(8,128)}, bf16[128,1024]{1,0:T(8,128)(2,1)S(1)}, bf16[128,1024]{1,0:T(8,128)(2,1)S(1)}, bf16[128,1024]{1,0:T(8,128)(2,1)S(1)}) custom-call(s32[1]{0:T(128)} %bitcast.me_ref, bf16[32,1,16,2048]{3,2,1,0:T(8,128)(2,1)} %bitcast.9.x_any.refs_4_, bf16[2048,1024]{1,0:T(8,128)(2,1)} %w_any.5), custom_call_target="tpu_custom_call" | custom-call | tf_op jit(solution)/shard_map/split_matmul/pallas_call | solution.py:100
  101.6 6.3 %collective-permute-done.12.refs_1_ = bf16[128,1024]{1,0:T(8,128)(2,1)S(1)} collective-permute-done((bf16[128,1024]{1,0:T(8,128)(2,1)S(1)}, bf16[128,1024]{1,0:T(8,128)(2,1)S(1)}, u32[]{:S(2)}, u32[]{:S(2)}) %collective-permute-start.12) | collective-permute-done | bytes 262176 | tf_op jit(solution)/shard_map/ppermute | solution.py:363
  107.9 5.2 %collective-permute-done.13.refs_2_ = bf16[128,1024]{1,0:T(8,128)(2,1)S(1)} collective-permute-done((bf16[128,1024]{1,0:T(8,128)(2,1)S(1)}, bf16[128,1024]{1,0:T(8,128)(2,1)S(1)}, u32[]{:S(2)}, u32[]{:S(2)}) %collective-permute-start.13) | collective-permute-done | bytes 262176 | tf_op jit(solution)/shard_map/ppermute | solution.py:363
  119.0 6.0 %collective-permute-done.17.refs_3_ = bf16[128,1024]{1,0:T(8,128)(2,1)S(1)} collective-permute-done((bf16[128,1024]{1,0:T(8,128)(2,1)S(1)}, bf16[128,1024]{1,0:T(8,128)(2,1)S(1)}, u32[]{:S(2)}, u32[]{:S(2)}) %collective-permute-start.17) | collective-permute-done | bytes 262176 | tf_op jit(solution)/shard_map/ppermute | solution.py:418
  126.8 6.3 %collective-permute-done.15.refs_1_ = bf16[128,1024]{1,0:T(8,128)(2,1)S(1)} collective-permute-done((bf16[128,1024]{1,0:T(8,128)(2,1)S(1)}, bf16[128,1024]{1,0:T(8,128)(2,1)S(1)}, u32[]{:S(2)}, u32[]{:S(2)}) %collective-permute-start.15) | collective-permute-done | bytes 262176 | tf_op jit(solution)/shard_map/ppermute | solution.py:418
  133.2 5.6 %decode.3 = (bf16[32,2,16,2048]{3,2,1,0:T(8,128)(2,1)}, bf16[512,1024]{1,0:T(8,128)(2,1)}) custom-call(s32[1]{0:T(128)} %bitcast.me_ref, bf16[128,1024]{1,0:T(8,128)(2,1)S(1)} %get-tuple-element.60.refs_0_, bf16[128,1024]{1,0:T(8,128)(2,1)S(1)} %collective-permute-done.15.refs_1_, bf16[128,1024]{1,0:T(8,128)(2,1)S(1)} %collective-permute-done.16.refs_2_, ...), custom_call_target="tpu_custom_call" | custom-call | tf_op jit(solution)/shard_map/decode/pallas_call | solution.py:150
  141.3 58.5 %all_to_all.25 = bf16[32,32,2048]{2,1,0:T(8,128)(2,1)} all-to-all(bf16[32,32,2048]{2,1,0:T(8,128)(2,1)} %bitcast.35), channel_id=1, replica_groups=mesh['dp'=4,'dict'=32] {'dict'}, dimensions={0} | all-to-all | bytes 8388608 | tf_op jit(solution)/shard_map/all_to_all | solution.py:356
  199.8 3.6 %residual_rows.3 = bf16[32,1,16,2048]{3,2,1,0:T(8,128)(2,1)} custom-call(bf16[512,128]{1,0:T(8,128)(2,1)S(1)} %fusion.sel_ref, bf16[32,2,16,2048]{3,2,1,0:T(8,128)(2,1)} %bitcast.32, bf16[16,16,2048]{2,1,0:T(8,128)(2,1)S(1)} %bitcast.25, f32[1,2048]{1,0:T(1,128)S(1)} %bitcast.28), custom_call_target="tpu_custom_call" | custom-call | tf_op jit(solution)/shard_map/residual_rows/pallas_call | solution.py:198
  203.3 3.9 %all-to-all-start.4 = ((bf16[32,16,2048]{2,1,0:T(8,128)(2,1)}), bf16[32,16,2048]{2,1,0:T(8,128)(2,1)S(1)}, u32[]{:S(2)}, u32[]{:S(2)}) async-start(bf16[32,16,2048]{2,1,0:T(8,128)(2,1)} %bitcast.36), calls=%async_computation.4 | async-start | bytes 4194304 | tf_op jit(solution)/shard_map/all_to_all | solution.py:356
  207.3 5.0 %split_matmul.9 = (f32[128,1024]{1,0:T(8,128)S(1)}, bf16[128,1024]{1,0:T(8,128)(2,1)S(1)}, bf16[128,1024]{1,0:T(8,128)(2,1)S(1)}, bf16[128,1024]{1,0:T(8,128)(2,1)S(1)}) custom-call(s32[1]{0:T(128)} %bitcast.me_ref, bf16[32,2,16,2048]{3,2,1,0:T(8,128)(2,1)} %bitcast.33, bf16[1024,2048]{1,0:T(8,128)(2,1)} %w_any.7), custom_call_target="tpu_custom_call" | custom-call | tf_op jit(solution)/shard_map/split_matmul/pallas_call | solution.py:100
  215.1 5.9 %outer_sum.3.refs_1_ = f32[1024,2048]{1,0:T(8,128)} custom-call(s32[1]{0:T(128)} %bitcast.me_ref, bf16[512,1024]{1,0:T(8,128)(2,1)S(1)} %copy-done.5, bf16[32,2,16,2048]{3,2,1,0:T(8,128)(2,1)} %bitcast.34), custom_call_target="tpu_custom_call" | custom-call | tf_op jit(solution)/shard_map/outer_sum/pallas_call | solution.py:282
  221.0 5.9 %collective-permute-done.18.refs_1_ = bf16[128,1024]{1,0:T(8,128)(2,1)S(1)} collective-permute-done((bf16[128,1024]{1,0:T(8,128)(2,1)S(1)}, bf16[128,1024]{1,0:T(8,128)(2,1)S(1)}, u32[]{:S(2)}, u32[]{:S(2)}) %collective-permute-start.18) | collective-permute-done | bytes 262176 | tf_op jit(solution)/shard_map/ppermute | solution.py:363
  230.7 4.9 %all-to-all-done.4 = bf16[32,16,2048]{2,1,0:T(8,128)(2,1)S(1)} async-done(((bf16[32,16,2048]{2,1,0:T(8,128)(2,1)}), bf16[32,16,2048]{2,1,0:T(8,128)(2,1)S(1)}, u32[]{:S(2)}, u32[]{:S(2)}) %all-to-all-start.4) | async-done | bytes 2097184 | tf_op jit(solution)/shard_map/all_to_all | solution.py:356
  235.6 3.4 %split_matmul.10 = (f32[64,1024]{1,0:T(8,128)S(1)}, bf16[64,1024]{1,0:T(8,128)(2,1)S(1)}, bf16[64,1024]{1,0:T(8,128)(2,1)S(1)}, bf16[64,1024]{1,0:T(8,128)(2,1)S(1)}, bf16[2,512,2048]{2,1,0:T(8,128)(2,1)S(1)}) custom-call(s32[1]{0:T(128)} %bitcast.me_ref, bf16[32,1,16,2048]{3,2,1,0:T(8,128)(2,1)S(1)} %bitcast.14, bf16[1024,2048]{1,0:T(8,128)(2,1)} %w_any.7), custom_call_target="tpu_custom_call" | custom-call | tf_op jit(solution)/shard_map/split_matmul/pallas_call | solution.py:100
  244.0 3.6 %collective-permute-done.30.refs_1_ = bf16[64,1024]{1,0:T(8,128)(2,1)S(1)} collective-permute-done((bf16[64,1024]{1,0:T(8,128)(2,1)S(1)}, bf16[64,1024]{1,0:T(8,128)(2,1)S(1)}, u32[]{:S(2)}, u32[]{:S(2)}) %collective-permute-start.30) | collective-permute-done | bytes 131104 | tf_op jit(solution)/shard_map/ppermute | solution.py:363
  257.1 3.3 %collective-permute-start.29 = (bf16[64,1024]{1,0:T(8,128)(2,1)S(1)}, bf16[64,1024]{1,0:T(8,128)(2,1)S(1)}, u32[]{:S(2)}, u32[]{:S(2)}) collective-permute-start(bf16[64,1024]{1,0:T(8,128)(2,1)S(1)} %grad_pre.4.refs_0_), channel_id=1, source_target_pairs={{0,96},{32,0},{64,32},{96,64},{1,97},{33,1},{65,33},{97,65},{2,98}... | collective-permute-start | bytes 393224 | tf_op jit(solution)/shard_map/ppermute | solution.py:418
  261.6 4.1 %outer_sum.5 = bf16[1024,2048]{1,0:T(8,128)(2,1)} custom-call(s32[1]{0:T(128)} %bitcast.me_ref, bf16[512,1024]{1,0:T(8,128)(2,1)S(1)} %copy-done.4, bf16[32,1,16,2048]{3,2,1,0:T(8,128)(2,1)S(1)} %bitcast.16, f32[1024,2048]{1,0:T(8,128)S(1)} %bitcast.21), custom_call_target="tpu_custom_call" | custom-call | tf_op jit(solution)/shard_map/outer_sum/pallas_call | solution.py:282
  269.8 4.3 %encoder_sum.1 = bf16[2048,1024]{1,0:T(8,128)(2,1)} custom-call(s32[1]{0:T(128)} %bitcast.me_ref, bf16[32,1,16,2048]{3,2,1,0:T(8,128)(2,1)S(1)} %get-tuple-element.70.left_ref, bf16[64,1024]{1,0:T(8,128)(2,1)S(1)} %grad_pre.4.refs_0_, bf16[64,1024]{1,0:T(8,128)(2,1)S(1)} %collective-permute-done.27.refs_1_, ...), custom_call_target="tpu_custom_call" | custom-call | tf_op jit(solution)/shard_map/encoder_sum/pallas_call | solution.py:313
  (120 shorter events, 74.5 us)
Async XLA Ops:
  5.0 37.8 %all-to-all-start = ((bf16[32,16,2048]{2,1,0:T(8,128)(2,1)}), bf16[32,16,2048]{2,1,0:T(8,128)(2,1)S(1)}, u32[]{:S(2)}, u32[]{:S(2)}) async-start(bf16[32,16,2048]{2,1,0:T(8,128)(2,1)} %bitcast.38), calls=%async_computation | async-start | bytes 4194304 | tf_op jit(solution)/shard_map/all_to_all | solution.py:356
  42.8 41.5 %all-to-all-start.2 = ((bf16[32,16,2048]{2,1,0:T(8,128)(2,1)}), bf16[32,16,2048]{2,1,0:T(8,128)(2,1)}, u32[]{:S(2)}, u32[]{:S(2)}) async-start(bf16[32,16,2048]{2,1,0:T(8,128)(2,1)} %bitcast.37), calls=%async_computation.2 | async-start | bytes 4194304 | tf_op jit(solution)/shard_map/all_to_all | solution.py:356
  52.5 8.7 %collective-permute-start.1 = (bf16[64,1024]{1,0:T(8,128)(2,1)S(1)}, bf16[64,1024]{1,0:T(8,128)(2,1)S(1)}, u32[]{:S(2)}, u32[]{:S(2)}) collective-permute-start(bf16[64,1024]{1,0:T(8,128)(2,1)S(1)} %get-tuple-element.45), channel_id=1, source_target_pairs={{0,64},{32,96},{64,0},{96,32},{1,65},{33,97},{65,1},{97,33},{2,66}... | collective-permute-start | bytes 393224 | tf_op jit(solution)/shard_map/ppermute | solution.py:363
  58.1 8.8 %collective-permute-start.7 = (bf16[64,1024]{1,0:T(8,128)(2,1)S(1)}, bf16[64,1024]{1,0:T(8,128)(2,1)S(1)}, u32[]{:S(2)}, u32[]{:S(2)}) collective-permute-start(bf16[64,1024]{1,0:T(8,128)(2,1)S(1)} %get-tuple-element.51), channel_id=1, source_target_pairs={{0,64},{32,96},{64,0},{96,32},{1,65},{33,97},{65,1},{97,33},{2,66}... | collective-permute-start | bytes 393224 | tf_op jit(solution)/shard_map/ppermute | solution.py:363
  62.0 8.6 %collective-permute-start.5 = (bf16[64,1024]{1,0:T(8,128)(2,1)S(1)}, bf16[64,1024]{1,0:T(8,128)(2,1)S(1)}, u32[]{:S(2)}, u32[]{:S(2)}) collective-permute-start(bf16[64,1024]{1,0:T(8,128)(2,1)S(1)} %get-tuple-element.47.refs_0_), channel_id=1, source_target_pairs={{0,96},{32,0},{64,32},{96,64},{1,97},{33,1},{65,33},{97,65},{2,98}... | collective-permute-start | bytes 393224 | tf_op jit(solution)/shard_map/ppermute | solution.py:418
  84.3 54.4 %all-to-all-start.1 = ((bf16[32,16,2048]{2,1,0:T(8,128)(2,1)}), bf16[32,16,2048]{2,1,0:T(8,128)(2,1)S(1)}, u32[]{:S(2)}, u32[]{:S(2)}) async-start(bf16[32,16,2048]{2,1,0:T(8,128)(2,1)} %bitcast.39), calls=%async_computation.1 | async-start | bytes 4194304 | tf_op jit(solution)/shard_map/all_to_all | solution.py:356
  98.8 9.1 %collective-permute-start.12 = (bf16[128,1024]{1,0:T(8,128)(2,1)S(1)}, bf16[128,1024]{1,0:T(8,128)(2,1)S(1)}, u32[]{:S(2)}, u32[]{:S(2)}) collective-permute-start(bf16[128,1024]{1,0:T(8,128)(2,1)S(1)} %get-tuple-element.57), channel_id=1, source_target_pairs={{0,32},{32,64},{64,96},{96,0},{1,33},{33,65},{65,97},{97,1},{2,34}... | collective-permute-start | bytes 786440 | tf_op jit(solution)/shard_map/ppermute | solution.py:363
  99.1 14.0 %collective-permute-start.13 = (bf16[128,1024]{1,0:T(8,128)(2,1)S(1)}, bf16[128,1024]{1,0:T(8,128)(2,1)S(1)}, u32[]{:S(2)}, u32[]{:S(2)}) collective-permute-start(bf16[128,1024]{1,0:T(8,128)(2,1)S(1)} %get-tuple-element.58), channel_id=1, source_target_pairs={{0,64},{32,96},{64,0},{96,32},{1,65},{33,97},{65,1},{97,33},{2,66}... | collective-permute-start | bytes 786440 | tf_op jit(solution)/shard_map/ppermute | solution.py:363
  101.3 12.4 %collective-permute-start.14 = (bf16[128,1024]{1,0:T(8,128)(2,1)S(1)}, bf16[128,1024]{1,0:T(8,128)(2,1)S(1)}, u32[]{:S(2)}, u32[]{:S(2)}) collective-permute-start(bf16[128,1024]{1,0:T(8,128)(2,1)S(1)} %get-tuple-element.59), channel_id=1, source_target_pairs={{0,96},{32,0},{64,32},{96,64},{1,97},{33,1},{65,33},{97,65},{2,98}... | collective-permute-start | bytes 786440 | tf_op jit(solution)/shard_map/ppermute | solution.py:363
  115.6 9.4 %collective-permute-start.17 = (bf16[128,1024]{1,0:T(8,128)(2,1)S(1)}, bf16[128,1024]{1,0:T(8,128)(2,1)S(1)}, u32[]{:S(2)}, u32[]{:S(2)}) collective-permute-start(bf16[128,1024]{1,0:T(8,128)(2,1)S(1)} %get-tuple-element.60.refs_0_), channel_id=1, source_target_pairs={{0,96},{32,0},{64,32},{96,64},{1,97},{33,1},{65,33},{97,65},{2,98}... | collective-permute-start | bytes 786440 | tf_op jit(solution)/shard_map/ppermute | solution.py:418
  118.4 14.8 %collective-permute-start.15 = (bf16[128,1024]{1,0:T(8,128)(2,1)S(1)}, bf16[128,1024]{1,0:T(8,128)(2,1)S(1)}, u32[]{:S(2)}, u32[]{:S(2)}) collective-permute-start(bf16[128,1024]{1,0:T(8,128)(2,1)S(1)} %get-tuple-element.60.refs_0_), channel_id=1, source_target_pairs={{0,32},{32,64},{64,96},{96,0},{1,33},{33,65},{65,97},{97,1},{2,34}... | collective-permute-start | bytes 786440 | tf_op jit(solution)/shard_map/ppermute | solution.py:418
  203.3 32.3 %all-to-all-start.4 = ((bf16[32,16,2048]{2,1,0:T(8,128)(2,1)}), bf16[32,16,2048]{2,1,0:T(8,128)(2,1)S(1)}, u32[]{:S(2)}, u32[]{:S(2)}) async-start(bf16[32,16,2048]{2,1,0:T(8,128)(2,1)} %bitcast.36), calls=%async_computation.4 | async-start | bytes 4194304 | tf_op jit(solution)/shard_map/all_to_all | solution.py:356
  212.3 14.5 %collective-permute-start.18 = (bf16[128,1024]{1,0:T(8,128)(2,1)S(1)}, bf16[128,1024]{1,0:T(8,128)(2,1)S(1)}, u32[]{:S(2)}, u32[]{:S(2)}) collective-permute-start(bf16[128,1024]{1,0:T(8,128)(2,1)S(1)} %get-tuple-element.65), channel_id=1, source_target_pairs={{0,32},{32,64},{64,96},{96,0},{1,33},{33,65},{65,97},{97,1},{2,34}... | collective-permute-start | bytes 786440 | tf_op jit(solution)/shard_map/ppermute | solution.py:363
  212.4 14.4 %collective-permute-start.19 = (bf16[128,1024]{1,0:T(8,128)(2,1)S(1)}, bf16[128,1024]{1,0:T(8,128)(2,1)S(1)}, u32[]{:S(2)}, u32[]{:S(2)}) collective-permute-start(bf16[128,1024]{1,0:T(8,128)(2,1)S(1)} %get-tuple-element.66), channel_id=1, source_target_pairs={{0,64},{32,96},{64,0},{96,32},{1,65},{33,97},{65,1},{97,33},{2,66}... | collective-permute-start | bytes 786440 | tf_op jit(solution)/shard_map/ppermute | solution.py:363
  214.2 13.0 %collective-permute-start.20 = (bf16[128,1024]{1,0:T(8,128)(2,1)S(1)}, bf16[128,1024]{1,0:T(8,128)(2,1)S(1)}, u32[]{:S(2)}, u32[]{:S(2)}) collective-permute-start(bf16[128,1024]{1,0:T(8,128)(2,1)S(1)} %get-tuple-element.67), channel_id=1, source_target_pairs={{0,96},{32,0},{64,32},{96,64},{1,97},{33,1},{65,33},{97,65},{2,98}... | collective-permute-start | bytes 786440 | tf_op jit(solution)/shard_map/ppermute | solution.py:363
  227.4 15.3 %collective-permute-start.23 = (bf16[128,1024]{1,0:T(8,128)(2,1)S(1)}, bf16[128,1024]{1,0:T(8,128)(2,1)S(1)}, u32[]{:S(2)}, u32[]{:S(2)}) collective-permute-start(bf16[128,1024]{1,0:T(8,128)(2,1)S(1)} %grad_pre.3.refs_0_), channel_id=1, source_target_pairs={{0,96},{32,0},{64,32},{96,64},{1,97},{33,1},{65,33},{97,65},{2,98}... | collective-permute-start | bytes 786440 | tf_op jit(solution)/shard_map/ppermute | solution.py:418
  230.1 22.8 %collective-permute-start.22 = (bf16[128,1024]{1,0:T(8,128)(2,1)S(1)}, bf16[128,1024]{1,0:T(8,128)(2,1)S(1)}, u32[]{:S(2)}, u32[]{:S(2)}) collective-permute-start(bf16[128,1024]{1,0:T(8,128)(2,1)S(1)} %grad_pre.3.refs_0_), channel_id=1, source_target_pairs={{0,64},{32,96},{64,0},{96,32},{1,65},{33,97},{65,1},{97,33},{2,66}... | collective-permute-start | bytes 786440 | tf_op jit(solution)/shard_map/ppermute | solution.py:418
  230.1 22.9 %collective-permute-start.21 = (bf16[128,1024]{1,0:T(8,128)(2,1)S(1)}, bf16[128,1024]{1,0:T(8,128)(2,1)S(1)}, u32[]{:S(2)}, u32[]{:S(2)}) collective-permute-start(bf16[128,1024]{1,0:T(8,128)(2,1)S(1)} %grad_pre.3.refs_0_), channel_id=1, source_target_pairs={{0,32},{32,64},{64,96},{96,0},{1,33},{33,65},{65,97},{97,1},{2,34}... | collective-permute-start | bytes 786440 | tf_op jit(solution)/shard_map/ppermute | solution.py:418
  240.8 8.6 %collective-permute-start.31 = (bf16[64,1024]{1,0:T(8,128)(2,1)S(1)}, bf16[64,1024]{1,0:T(8,128)(2,1)S(1)}, u32[]{:S(2)}, u32[]{:S(2)}) collective-permute-start(bf16[64,1024]{1,0:T(8,128)(2,1)S(1)} %get-tuple-element.81), channel_id=1, source_target_pairs={{0,64},{32,96},{64,0},{96,32},{1,65},{33,97},{65,1},{97,33},{2,66}... | collective-permute-start | bytes 393224 | tf_op jit(solution)/shard_map/ppermute | solution.py:363
  247.6 9.1 %collective-permute-start.24 = (bf16[64,1024]{1,0:T(8,128)(2,1)S(1)}, bf16[64,1024]{1,0:T(8,128)(2,1)S(1)}, u32[]{:S(2)}, u32[]{:S(2)}) collective-permute-start(bf16[64,1024]{1,0:T(8,128)(2,1)S(1)} %get-tuple-element.74), channel_id=1, source_target_pairs={{0,32},{32,64},{64,96},{96,0},{1,33},{33,65},{65,97},{97,1},{2,34}... | collective-permute-start | bytes 393224 | tf_op jit(solution)/shard_map/ppermute | solution.py:363
  255.5 10.2 %collective-permute-start.34 = (bf16[64,1024]{1,0:T(8,128)(2,1)S(1)}, bf16[64,1024]{1,0:T(8,128)(2,1)S(1)}, u32[]{:S(2)}, u32[]{:S(2)}) collective-permute-start(bf16[64,1024]{1,0:T(8,128)(2,1)S(1)} %grad_pre.5.refs_4_), channel_id=1, source_target_pairs={{0,64},{32,96},{64,0},{96,32},{1,65},{33,97},{65,1},{97,33},{2,66}... | collective-permute-start | bytes 393224 | tf_op jit(solution)/shard_map/ppermute | solution.py:418
  256.6 9.0 %collective-permute-start.33 = (bf16[64,1024]{1,0:T(8,128)(2,1)S(1)}, bf16[64,1024]{1,0:T(8,128)(2,1)S(1)}, u32[]{:S(2)}, u32[]{:S(2)}) collective-permute-start(bf16[64,1024]{1,0:T(8,128)(2,1)S(1)} %grad_pre.5.refs_4_), channel_id=1, source_target_pairs={{0,32},{32,64},{64,96},{96,0},{1,33},{33,65},{65,97},{97,1},{2,34}... | collective-permute-start | bytes 393224 | tf_op jit(solution)/shard_map/ppermute | solution.py:418
  257.1 9.4 %collective-permute-start.29 = (bf16[64,1024]{1,0:T(8,128)(2,1)S(1)}, bf16[64,1024]{1,0:T(8,128)(2,1)S(1)}, u32[]{:S(2)}, u32[]{:S(2)}) collective-permute-start(bf16[64,1024]{1,0:T(8,128)(2,1)S(1)} %grad_pre.4.refs_0_), channel_id=1, source_target_pairs={{0,96},{32,0},{64,32},{96,64},{1,97},{33,1},{65,33},{97,65},{2,98}... | collective-permute-start | bytes 393224 | tf_op jit(solution)/shard_map/ppermute | solution.py:418
  260.9 8.9 %collective-permute-start.27 = (bf16[64,1024]{1,0:T(8,128)(2,1)S(1)}, bf16[64,1024]{1,0:T(8,128)(2,1)S(1)}, u32[]{:S(2)}, u32[]{:S(2)}) collective-permute-start(bf16[64,1024]{1,0:T(8,128)(2,1)S(1)} %grad_pre.4.refs_0_), channel_id=1, source_target_pairs={{0,32},{32,64},{64,96},{96,0},{1,33},{33,65},{65,97},{97,1},{2,34}... | collective-permute-start | bytes 393224 | tf_op jit(solution)/shard_map/ppermute | solution.py:418
  (29 other events, 334.6 us)

commit v4 on v3

--- a/solution.py
+++ b/solution.py
@@ -40,7 +40,7 @@
     return pl.BlockSpec(memory_space=VMEM)
 
 
-def split_matmul(me, rows4, lane, half, weight, transposed, size, tile=512, keep=False, kept=False, away=False):
+def split_matmul(me, rows4, lane, half, weight, transposed, size, tile=512, keep=False, kept=False, away=False, wire=BF16):
     peers, _, slot_rows, inner = rows4.shape
     halves = 2 if half is None else 1
     my_peers = peers * halves // 2
@@ -95,7 +95,7 @@
 
             own_ref[to, :] = piece(mine)
             for shift in range(1, size):
-                sends[shift - 1][to, :] = piece(lax.rem(mine + shift, size)).astype(BF16)
+                sends[shift - 1][to, :] = piece(lax.rem(mine + shift, size)).astype(wire)
 
     return pl.pallas_call(
         body,
@@ -107,7 +107,7 @@
         out_specs=[pl.BlockSpec((halves * quarter, outer), lambda: (0, 0)) if away else whole()]
         + [whole()] * (size - 1 + (1 if keep else 0)),
         out_shape=[(pltpu.HBM if away else jax.ShapeDtypeStruct)((halves * quarter, outer), F32)]
-        + [jax.ShapeDtypeStruct((halves * quarter, outer), BF16)] * (size - 1)
+        + [jax.ShapeDtypeStruct((halves * quarter, outer), wire)] * (size - 1)
         + ([VMEM(tiles, BF16)] if keep else []),
         scratch_shapes=[
             pltpu.VMEM((count, outer), F32),
@@ -452,14 +452,21 @@
     w_dec = far(w_dec)
 
     def share(rows4, lane, weight, transposed, away=False):
-        return split_matmul(me, rows4, lane, None, weight, transposed, size, away=away)
+        wire = BF16 if transposed else F32
+        return split_matmul(
+            me, rows4, lane, None, weight, transposed, size, away=away, wire=wire
+        )
 
     def first_half(rows4, weight, transposed):
-        *pieces, tiles = split_matmul(me, rows4, 0, 0, weight, transposed, size, keep=True)
+        wire = BF16 if transposed else F32
+        *pieces, tiles = split_matmul(
+            me, rows4, 0, 0, weight, transposed, size, keep=True, wire=wire
+        )
         return pieces, tiles
 
     def second_half(rows4, tiles, transposed):
-        return split_matmul(me, rows4, 0, 1, tiles, transposed, size, kept=True)
+        wire = BF16 if transposed else F32
+        return split_matmul(me, rows4, 0, 1, tiles, transposed, size, kept=True, wire=wire)
 
 
     in_a = exchange(dispatch(selector, far(blocks), 0, peers))

time: 277 us -> 299 us (1.079)
  waiting for transfers between devices: 83.2 us -> 105 us
    ppermute x18, waiting for transfers between devices: 26.3 us -> 48 us  [swap_pieces(): out.append(lax.ppermute(pieces[shift], 'dp', ring(size, shift)))]
  transfers between devices with their start and end apart: 40 -> 40, of which waited for: 22 -> 23; matrix products, arithmetic and copies ran while one was open for 0% -> 0% of each run, Pallas kernels for 18% -> 17%
where the time goes in v4:
time: 299 us; the launch traced here: 296 us
  waiting for transfers between devices  105 us (35%)
  starting transfers between devices  67.2 us (22%)
  Pallas kernels  62.2 us (21%)
  blocking collectives  58.5 us (20%)
    all_to_all x1, blocking collectives, exchange(): got = lax.all_to_all(flat, 'dict', split_axis=0, concat_axis=0, tiled=True)  58.5 us
    ppermute x18, waiting for transfers between devices, swap_pieces(): out.append(lax.ppermute(pieces[shift], 'dp', ring(size, shift)))  48 us
    all_to_all x4, waiting for transfers between devices, exchange(): got = lax.all_to_all(flat, 'dict', split_axis=0, concat_axis=0, tiled=True)  30.4 us
    all_to_all x4, starting transfers between devices, exchange(): got = lax.all_to_all(flat, 'dict', split_axis=0, concat_axis=0, tiled=True)  26.8 us
    ppermute x18, waiting for transfers between devices, spread(): out.append(lax.ppermute(own, 'dp', ring(size, shift)))  26.4 us
    ppermute x18, starting transfers between devices, swap_pieces(): out.append(lax.ppermute(pieces[shift], 'dp', ring(size, shift)))  20.6 us
    pallas_call x6, Pallas kernels, split_matmul(): pl.pallas_call(body, in_specs=[pl.BlockSpec(memory_space=pltpu.SMEM), pl....  20.2 us
    ppermute x18, starting transfers between devices, spread(): out.append(lax.ppermute(own, 'dp', ring(size, shift)))  19.8 us
  transfers between devices with their start and end apart: 40, of which 23 were waited for; matrix products, arithmetic and copies ran while one was open for 0% of the time, Pallas kernels for 17%

profile of v4, /device:TPU:1, one launch (start us, length us, event | category | flops | bytes accessed | tf_op | source)
XLA Modules:
  0.0 296.3 jit_solution(10715033433624585591)
XLA Ops:
  5.0 9.4 %all-to-all-start = ((bf16[32,16,2048]{2,1,0:T(8,128)(2,1)}), bf16[32,16,2048]{2,1,0:T(8,128)(2,1)S(1)}, u32[]{:S(2)}, u32[]{:S(2)}) async-start(bf16[32,16,2048]{2,1,0:T(8,128)(2,1)} %bitcast.38), calls=%async_computation | async-start | bytes 4194304 | tf_op jit(solution)/shard_map/all_to_all | solution.py:356
  17.3 25.5 %all-to-all-done = bf16[32,16,2048]{2,1,0:T(8,128)(2,1)S(1)} async-done(((bf16[32,16,2048]{2,1,0:T(8,128)(2,1)}), bf16[32,16,2048]{2,1,0:T(8,128)(2,1)S(1)}, u32[]{:S(2)}, u32[]{:S(2)}) %all-to-all-start) | async-done | bytes 2097184 | tf_op jit(solution)/shard_map/all_to_all | solution.py:356
  42.8 5.2 %all-to-all-start.2 = ((bf16[32,16,2048]{2,1,0:T(8,128)(2,1)}), bf16[32,16,2048]{2,1,0:T(8,128)(2,1)}, u32[]{:S(2)}, u32[]{:S(2)}) async-start(bf16[32,16,2048]{2,1,0:T(8,128)(2,1)} %bitcast.37), calls=%async_computation.2 | async-start | bytes 4194304 | tf_op jit(solution)/shard_map/all_to_all | solution.py:356
  61.5 5.4 %collective-permute-done.1.refs_2_ = f32[64,1024]{1,0:T(8,128)S(1)} collective-permute-done((f32[64,1024]{1,0:T(8,128)S(1)}, f32[64,1024]{1,0:T(8,128)S(1)}, u32[]{:S(2)}, u32[]{:S(2)}) %collective-permute-start.1) | collective-permute-done | bytes 262176 | tf_op jit(solution)/shard_map/ppermute | solution.py:363
  67.7 3.5 %collective-permute-start.5 = (bf16[64,1024]{1,0:T(8,128)(2,1)S(1)}, bf16[64,1024]{1,0:T(8,128)(2,1)S(1)}, u32[]{:S(2)}, u32[]{:S(2)}) collective-permute-start(bf16[64,1024]{1,0:T(8,128)(2,1)S(1)} %get-tuple-element.47.refs_0_), channel_id=1, source_target_pairs={{0,96},{32,0},{64,32},{96,64},{1,97},{33,1},{65,33},{97,65},{2,98}... | collective-permute-start | bytes 393224 | tf_op jit(solution)/shard_map/ppermute | solution.py:418
  72.0 6.1 %collective-permute-done.7.refs_2_ = f32[64,1024]{1,0:T(8,128)S(1)} collective-permute-done((f32[64,1024]{1,0:T(8,128)S(1)}, f32[64,1024]{1,0:T(8,128)S(1)}, u32[]{:S(2)}, u32[]{:S(2)}) %collective-permute-start.7) | collective-permute-done | bytes 262176 | tf_op jit(solution)/shard_map/ppermute | solution.py:363
  90.3 5.2 %decode.2 = (bf16[32,1,16,2048]{3,2,1,0:T(8,128)(2,1)}, bf16[512,1024]{1,0:T(8,128)(2,1)}) custom-call(s32[1]{0:T(128)} %bitcast.me_ref, bf16[64,1024]{1,0:T(8,128)(2,1)S(1)} %get-tuple-element.47.refs_0_, bf16[64,1024]{1,0:T(8,128)(2,1)S(1)} %collective-permute-done.3.refs_1_, bf16[64,1024]{1,0:T(8,128)(2,1)S(1)} %collective-permute-done.4.refs_2_, ...), custom_call_target="tpu_custom_call" | custom-call | tf_op jit(solution)/shard_map/decode/pallas_call | solution.py:150
  95.6 8.3 %all-to-all-start.1 = ((bf16[32,16,2048]{2,1,0:T(8,128)(2,1)}), bf16[32,16,2048]{2,1,0:T(8,128)(2,1)S(1)}, u32[]{:S(2)}, u32[]{:S(2)}) async-start(bf16[32,16,2048]{2,1,0:T(8,128)(2,1)} %bitcast.39), calls=%async_computation.1 | async-start | bytes 4194304 | tf_op jit(solution)/shard_map/all_to_all | solution.py:356
  103.9 5.7 %split_matmul.8 = (f32[128,1024]{1,0:T(8,128)}, f32[128,1024]{1,0:T(8,128)S(1)}, f32[128,1024]{1,0:T(8,128)S(1)}, f32[128,1024]{1,0:T(8,128)S(1)}) custom-call(s32[1]{0:T(128)} %bitcast.me_ref, bf16[32,1,16,2048]{3,2,1,0:T(8,128)(2,1)} %bitcast.9.x_any.refs_4_, bf16[2048,1024]{1,0:T(8,128)(2,1)} %w_any.5), custom_call_target="tpu_custom_call" | custom-call | tf_op jit(solution)/shard_map/split_matmul/pallas_call | solution.py:100
  112.9 11.8 %collective-permute-done.12.refs_1_ = f32[128,1024]{1,0:T(8,128)S(1)} collective-permute-done((f32[128,1024]{1,0:T(8,128)S(1)}, f32[128,1024]{1,0:T(8,128)S(1)}, u32[]{:S(2)}, u32[]{:S(2)}) %collective-permute-start.12) | collective-permute-done | bytes 524320 | tf_op jit(solution)/shard_map/ppermute | solution.py:363
  124.6 10.2 %collective-permute-done.13.refs_2_ = f32[128,1024]{1,0:T(8,128)S(1)} collective-permute-done((f32[128,1024]{1,0:T(8,128)S(1)}, f32[128,1024]{1,0:T(8,128)S(1)}, u32[]{:S(2)}, u32[]{:S(2)}) %collective-permute-start.13) | collective-permute-done | bytes 524320 | tf_op jit(solution)/shard_map/ppermute | solution.py:363
  141.5 10.1 %collective-permute-done.17.refs_3_ = bf16[128,1024]{1,0:T(8,128)(2,1)S(1)} collective-permute-done((bf16[128,1024]{1,0:T(8,128)(2,1)S(1)}, bf16[128,1024]{1,0:T(8,128)(2,1)S(1)}, u32[]{:S(2)}, u32[]{:S(2)}) %collective-permute-start.17) | collective-permute-done | bytes 262176 | tf_op jit(solution)/shard_map/ppermute | solution.py:418
  151.5 4.1 %collective-permute-done.15.refs_1_ = bf16[128,1024]{1,0:T(8,128)(2,1)S(1)} collective-permute-done((bf16[128,1024]{1,0:T(8,128)(2,1)S(1)}, bf16[128,1024]{1,0:T(8,128)(2,1)S(1)}, u32[]{:S(2)}, u32[]{:S(2)}) %collective-permute-start.15) | collective-permute-done | bytes 262176 | tf_op jit(solution)/shard_map/ppermute | solution.py:418
  155.6 5.6 %decode.3 = (bf16[32,2,16,2048]{3,2,1,0:T(8,128)(2,1)}, bf16[512,1024]{1,0:T(8,128)(2,1)}) custom-call(s32[1]{0:T(128)} %bitcast.me_ref, bf16[128,1024]{1,0:T(8,128)(2,1)S(1)} %get-tuple-element.60.refs_0_, bf16[128,1024]{1,0:T(8,128)(2,1)S(1)} %collective-permute-done.15.refs_1_, bf16[128,1024]{1,0:T(8,128)(2,1)S(1)} %collective-permute-done.16.refs_2_, ...), custom_call_target="tpu_custom_call" | custom-call | tf_op jit(solution)/shard_map/decode/pallas_call | solution.py:150
  163.8 58.5 %all_to_all.25 = bf16[32,32,2048]{2,1,0:T(8,128)(2,1)} all-to-all(bf16[32,32,2048]{2,1,0:T(8,128)(2,1)} %bitcast.35), channel_id=1, replica_groups=mesh['dp'=4,'dict'=32] {'dict'}, dimensions={0} | all-to-all | bytes 8388608 | tf_op jit(solution)/shard_map/all_to_all | solution.py:356
  222.2 3.6 %residual_rows.3 = bf16[32,1,16,2048]{3,2,1,0:T(8,128)(2,1)} custom-call(bf16[512,128]{1,0:T(8,128)(2,1)S(1)} %fusion.sel_ref, bf16[32,2,16,2048]{3,2,1,0:T(8,128)(2,1)} %bitcast.32, bf16[16,16,2048]{2,1,0:T(8,128)(2,1)S(1)} %bitcast.25, f32[1,2048]{1,0:T(1,128)S(1)} %bitcast.28), custom_call_target="tpu_custom_call" | custom-call | tf_op jit(solution)/shard_map/residual_rows/pallas_call | solution.py:198
  225.8 3.9 %all-to-all-start.4 = ((bf16[32,16,2048]{2,1,0:T(8,128)(2,1)}), bf16[32,16,2048]{2,1,0:T(8,128)(2,1)S(1)}, u32[]{:S(2)}, u32[]{:S(2)}) async-start(bf16[32,16,2048]{2,1,0:T(8,128)(2,1)} %bitcast.36), calls=%async_computation.4 | async-start | bytes 4194304 | tf_op jit(solution)/shard_map/all_to_all | solution.py:356
  229.8 5.0 %split_matmul.9 = (f32[128,1024]{1,0:T(8,128)S(1)}, bf16[128,1024]{1,0:T(8,128)(2,1)S(1)}, bf16[128,1024]{1,0:T(8,128)(2,1)S(1)}, bf16[128,1024]{1,0:T(8,128)(2,1)S(1)}) custom-call(s32[1]{0:T(128)} %bitcast.me_ref, bf16[32,2,16,2048]{3,2,1,0:T(8,128)(2,1)} %bitcast.33, bf16[1024,2048]{1,0:T(8,128)(2,1)} %w_any.7), custom_call_target="tpu_custom_call" | custom-call | tf_op jit(solution)/shard_map/split_matmul/pallas_call | solution.py:100
  237.6 5.9 %outer_sum.3.refs_1_ = f32[1024,2048]{1,0:T(8,128)} custom-call(s32[1]{0:T(128)} %bitcast.me_ref, bf16[512,1024]{1,0:T(8,128)(2,1)S(1)} %copy-done.5, bf16[32,2,16,2048]{3,2,1,0:T(8,128)(2,1)} %bitcast.34), custom_call_target="tpu_custom_call" | custom-call | tf_op jit(solution)/shard_map/outer_sum/pallas_call | solution.py:282
  243.5 5.9 %collective-permute-done.18.refs_1_ = bf16[128,1024]{1,0:T(8,128)(2,1)S(1)} collective-permute-done((bf16[128,1024]{1,0:T(8,128)(2,1)S(1)}, bf16[128,1024]{1,0:T(8,128)(2,1)S(1)}, u32[]{:S(2)}, u32[]{:S(2)}) %collective-permute-start.18) | collective-permute-done | bytes 262176 | tf_op jit(solution)/shard_map/ppermute | solution.py:363
  253.2 4.9 %all-to-all-done.4 = bf16[32,16,2048]{2,1,0:T(8,128)(2,1)S(1)} async-done(((bf16[32,16,2048]{2,1,0:T(8,128)(2,1)}), bf16[32,16,2048]{2,1,0:T(8,128)(2,1)S(1)}, u32[]{:S(2)}, u32[]{:S(2)}) %all-to-all-start.4) | async-done | bytes 2097184 | tf_op jit(solution)/shard_map/all_to_all | solution.py:356
  266.5 3.6 %collective-permute-done.30.refs_1_ = bf16[64,1024]{1,0:T(8,128)(2,1)S(1)} collective-permute-done((bf16[64,1024]{1,0:T(8,128)(2,1)S(1)}, bf16[64,1024]{1,0:T(8,128)(2,1)S(1)}, u32[]{:S(2)}, u32[]{:S(2)}) %collective-permute-start.30) | collective-permute-done | bytes 131104 | tf_op jit(solution)/shard_map/ppermute | solution.py:363
  284.1 4.1 %outer_sum.5 = bf16[1024,2048]{1,0:T(8,128)(2,1)} custom-call(s32[1]{0:T(128)} %bitcast.me_ref, bf16[512,1024]{1,0:T(8,128)(2,1)S(1)} %copy-done.4, bf16[32,1,16,2048]{3,2,1,0:T(8,128)(2,1)S(1)} %bitcast.16, f32[1024,2048]{1,0:T(8,128)S(1)} %bitcast.21), custom_call_target="tpu_custom_call" | custom-call | tf_op jit(solution)/shard_map/outer_sum/pallas_call | solution.py:282
  292.0 4.3 %encoder_sum.1 = bf16[2048,1024]{1,0:T(8,128)(2,1)} custom-call(s32[1]{0:T(128)} %bitcast.me_ref, bf16[32,1,16,2048]{3,2,1,0:T(8,128)(2,1)S(1)} %get-tuple-element.70.left_ref, bf16[64,1024]{1,0:T(8,128)(2,1)S(1)} %grad_pre.4.refs_0_, bf16[64,1024]{1,0:T(8,128)(2,1)S(1)} %collective-permute-done.27.refs_1_, ...), custom_call_target="tpu_custom_call" | custom-call | tf_op jit(solution)/shard_map/encoder_sum/pallas_call | solution.py:313
  (120 shorter events, 79.7 us)
Async XLA Ops:
  5.0 37.8 %all-to-all-start = ((bf16[32,16,2048]{2,1,0:T(8,128)(2,1)}), bf16[32,16,2048]{2,1,0:T(8,128)(2,1)S(1)}, u32[]{:S(2)}, u32[]{:S(2)}) async-start(bf16[32,16,2048]{2,1,0:T(8,128)(2,1)} %bitcast.38), calls=%async_computation | async-start | bytes 4194304 | tf_op jit(solution)/shard_map/all_to_all | solution.py:356
  42.8 52.8 %all-to-all-start.2 = ((bf16[32,16,2048]{2,1,0:T(8,128)(2,1)}), bf16[32,16,2048]{2,1,0:T(8,128)(2,1)}, u32[]{:S(2)}, u32[]{:S(2)}) async-start(bf16[32,16,2048]{2,1,0:T(8,128)(2,1)} %bitcast.37), calls=%async_computation.2 | async-start | bytes 4194304 | tf_op jit(solution)/shard_map/all_to_all | solution.py:356
  52.5 14.4 %collective-permute-start.1 = (f32[64,1024]{1,0:T(8,128)S(1)}, f32[64,1024]{1,0:T(8,128)S(1)}, u32[]{:S(2)}, u32[]{:S(2)}) collective-permute-start(f32[64,1024]{1,0:T(8,128)S(1)} %get-tuple-element.45), channel_id=1, source_target_pairs={{0,64},{32,96},{64,0},{96,32},{1,65},{33,97},{65,1},{97,33},{2,66}... | collective-permute-start | bytes 786440 | tf_op jit(solution)/shard_map/ppermute | solution.py:363
  55.2 11.7 %collective-permute-start.2 = (f32[64,1024]{1,0:T(8,128)S(1)}, f32[64,1024]{1,0:T(8,128)S(1)}, u32[]{:S(2)}, u32[]{:S(2)}) collective-permute-start(f32[64,1024]{1,0:T(8,128)S(1)} %get-tuple-element.46), channel_id=1, source_target_pairs={{0,96},{32,0},{64,32},{96,64},{1,97},{33,1},{65,33},{97,65},{2,98}... | collective-permute-start | bytes 786440 | tf_op jit(solution)/shard_map/ppermute | solution.py:363
  57.7 14.3 %collective-permute-start.6 = (f32[64,1024]{1,0:T(8,128)S(1)}, f32[64,1024]{1,0:T(8,128)S(1)}, u32[]{:S(2)}, u32[]{:S(2)}) collective-permute-start(f32[64,1024]{1,0:T(8,128)S(1)} %get-tuple-element.50), channel_id=1, source_target_pairs={{0,32},{32,64},{64,96},{96,0},{1,33},{33,65},{65,97},{97,1},{2,34}... | collective-permute-start | bytes 786440 | tf_op jit(solution)/shard_map/ppermute | solution.py:363
  58.1 20.0 %collective-permute-start.7 = (f32[64,1024]{1,0:T(8,128)S(1)}, f32[64,1024]{1,0:T(8,128)S(1)}, u32[]{:S(2)}, u32[]{:S(2)}) collective-permute-start(f32[64,1024]{1,0:T(8,128)S(1)} %get-tuple-element.51), channel_id=1, source_target_pairs={{0,64},{32,96},{64,0},{96,32},{1,65},{33,97},{65,1},{97,33},{2,66}... | collective-permute-start | bytes 786440 | tf_op jit(solution)/shard_map/ppermute | solution.py:363
  60.1 17.9 %collective-permute-start.8 = (f32[64,1024]{1,0:T(8,128)S(1)}, f32[64,1024]{1,0:T(8,128)S(1)}, u32[]{:S(2)}, u32[]{:S(2)}) collective-permute-start(f32[64,1024]{1,0:T(8,128)S(1)} %get-tuple-element.52), channel_id=1, source_target_pairs={{0,96},{32,0},{64,32},{96,64},{1,97},{33,1},{65,33},{97,65},{2,98}... | collective-permute-start | bytes 786440 | tf_op jit(solution)/shard_map/ppermute | solution.py:363
  67.7 13.9 %collective-permute-start.5 = (bf16[64,1024]{1,0:T(8,128)(2,1)S(1)}, bf16[64,1024]{1,0:T(8,128)(2,1)S(1)}, u32[]{:S(2)}, u32[]{:S(2)}) collective-permute-start(bf16[64,1024]{1,0:T(8,128)(2,1)S(1)} %get-tuple-element.47.refs_0_), channel_id=1, source_target_pairs={{0,96},{32,0},{64,32},{96,64},{1,97},{33,1},{65,33},{97,65},{2,98}... | collective-permute-start | bytes 393224 | tf_op jit(solution)/shard_map/ppermute | solution.py:418
  71.2 10.9 %collective-permute-start.4 = (bf16[64,1024]{1,0:T(8,128)(2,1)S(1)}, bf16[64,1024]{1,0:T(8,128)(2,1)S(1)}, u32[]{:S(2)}, u32[]{:S(2)}) collective-permute-start(bf16[64,1024]{1,0:T(8,128)(2,1)S(1)} %get-tuple-element.47.refs_0_), channel_id=1, source_target_pairs={{0,64},{32,96},{64,0},{96,32},{1,65},{33,97},{65,1},{97,33},{2,66}... | collective-permute-start | bytes 393224 | tf_op jit(solution)/shard_map/ppermute | solution.py:418
  72.0 12.4 %collective-permute-start.3 = (bf16[64,1024]{1,0:T(8,128)(2,1)S(1)}, bf16[64,1024]{1,0:T(8,128)(2,1)S(1)}, u32[]{:S(2)}, u32[]{:S(2)}) collective-permute-start(bf16[64,1024]{1,0:T(8,128)(2,1)S(1)} %get-tuple-element.47.refs_0_), channel_id=1, source_target_pairs={{0,32},{32,64},{64,96},{96,0},{1,33},{33,65},{65,97},{97,1},{2,34}... | collective-permute-start | bytes 393224 | tf_op jit(solution)/shard_map/ppermute | solution.py:418
  95.6 65.6 %all-to-all-start.1 = ((bf16[32,16,2048]{2,1,0:T(8,128)(2,1)}), bf16[32,16,2048]{2,1,0:T(8,128)(2,1)S(1)}, u32[]{:S(2)}, u32[]{:S(2)}) async-start(bf16[32,16,2048]{2,1,0:T(8,128)(2,1)} %bitcast.39), calls=%async_computation.1 | async-start | bytes 4194304 | tf_op jit(solution)/shard_map/all_to_all | solution.py:356
  109.6 15.0 %collective-permute-start.12 = (f32[128,1024]{1,0:T(8,128)S(1)}, f32[128,1024]{1,0:T(8,128)S(1)}, u32[]{:S(2)}, u32[]{:S(2)}) collective-permute-start(f32[128,1024]{1,0:T(8,128)S(1)} %get-tuple-element.57), channel_id=1, source_target_pairs={{0,32},{32,64},{64,96},{96,0},{1,33},{33,65},{65,97},{97,1},{2,34}... | collective-permute-start | bytes 1572872 | tf_op jit(solution)/shard_map/ppermute | solution.py:363
  110.4 24.5 %collective-permute-start.13 = (f32[128,1024]{1,0:T(8,128)S(1)}, f32[128,1024]{1,0:T(8,128)S(1)}, u32[]{:S(2)}, u32[]{:S(2)}) collective-permute-start(f32[128,1024]{1,0:T(8,128)S(1)} %get-tuple-element.58), channel_id=1, source_target_pairs={{0,64},{32,96},{64,0},{96,32},{1,65},{33,97},{65,1},{97,33},{2,66}... | collective-permute-start | bytes 1572872 | tf_op jit(solution)/shard_map/ppermute | solution.py:363
  111.8 23.9 %collective-permute-start.14 = (f32[128,1024]{1,0:T(8,128)S(1)}, f32[128,1024]{1,0:T(8,128)S(1)}, u32[]{:S(2)}, u32[]{:S(2)}) collective-permute-start(f32[128,1024]{1,0:T(8,128)S(1)} %get-tuple-element.59), channel_id=1, source_target_pairs={{0,96},{32,0},{64,32},{96,64},{1,97},{33,1},{65,33},{97,65},{2,98}... | collective-permute-start | bytes 1572872 | tf_op jit(solution)/shard_map/ppermute | solution.py:363
  137.6 13.9 %collective-permute-start.17 = (bf16[128,1024]{1,0:T(8,128)(2,1)S(1)}, bf16[128,1024]{1,0:T(8,128)(2,1)S(1)}, u32[]{:S(2)}, u32[]{:S(2)}) collective-permute-start(bf16[128,1024]{1,0:T(8,128)(2,1)S(1)} %get-tuple-element.60.refs_0_), channel_id=1, source_target_pairs={{0,96},{32,0},{64,32},{96,64},{1,97},{33,1},{65,33},{97,65},{2,98}... | collective-permute-start | bytes 786440 | tf_op jit(solution)/shard_map/ppermute | solution.py:418
  140.9 10.7 %collective-permute-start.16 = (bf16[128,1024]{1,0:T(8,128)(2,1)S(1)}, bf16[128,1024]{1,0:T(8,128)(2,1)S(1)}, u32[]{:S(2)}, u32[]{:S(2)}) collective-permute-start(bf16[128,1024]{1,0:T(8,128)(2,1)S(1)} %get-tuple-element.60.refs_0_), channel_id=1, source_target_pairs={{0,64},{32,96},{64,0},{96,32},{1,65},{33,97},{65,1},{97,33},{2,66}... | collective-permute-start | bytes 786440 | tf_op jit(solution)/shard_map/ppermute | solution.py:418
  140.9 14.8 %collective-permute-start.15 = (bf16[128,1024]{1,0:T(8,128)(2,1)S(1)}, bf16[128,1024]{1,0:T(8,128)(2,1)S(1)}, u32[]{:S(2)}, u32[]{:S(2)}) collective-permute-start(bf16[128,1024]{1,0:T(8,128)(2,1)S(1)} %get-tuple-element.60.refs_0_), channel_id=1, source_target_pairs={{0,32},{32,64},{64,96},{96,0},{1,33},{33,65},{65,97},{97,1},{2,34}... | collective-permute-start | bytes 786440 | tf_op jit(solution)/shard_map/ppermute | solution.py:418
  225.8 32.3 %all-to-all-start.4 = ((bf16[32,16,2048]{2,1,0:T(8,128)(2,1)}), bf16[32,16,2048]{2,1,0:T(8,128)(2,1)S(1)}, u32[]{:S(2)}, u32[]{:S(2)}) async-start(bf16[32,16,2048]{2,1,0:T(8,128)(2,1)} %bitcast.36), calls=%async_computation.4 | async-start | bytes 4194304 | tf_op jit(solution)/shard_map/all_to_all | solution.py:356
  234.8 14.5 %collective-permute-start.18 = (bf16[128,1024]{1,0:T(8,128)(2,1)S(1)}, bf16[128,1024]{1,0:T(8,128)(2,1)S(1)}, u32[]{:S(2)}, u32[]{:S(2)}) collective-permute-start(bf16[128,1024]{1,0:T(8,128)(2,1)S(1)} %get-tuple-element.65), channel_id=1, source_target_pairs={{0,32},{32,64},{64,96},{96,0},{1,33},{33,65},{65,97},{97,1},{2,34}... | collective-permute-start | bytes 786440 | tf_op jit(solution)/shard_map/ppermute | solution.py:363
  234.9 14.4 %collective-permute-start.19 = (bf16[128,1024]{1,0:T(8,128)(2,1)S(1)}, bf16[128,1024]{1,0:T(8,128)(2,1)S(1)}, u32[]{:S(2)}, u32[]{:S(2)}) collective-permute-start(bf16[128,1024]{1,0:T(8,128)(2,1)S(1)} %get-tuple-element.66), channel_id=1, source_target_pairs={{0,64},{32,96},{64,0},{96,32},{1,65},{33,97},{65,1},{97,33},{2,66}... | collective-permute-start | bytes 786440 | tf_op jit(solution)/shard_map/ppermute | solution.py:363
  236.7 13.0 %collective-permute-start.20 = (bf16[128,1024]{1,0:T(8,128)(2,1)S(1)}, bf16[128,1024]{1,0:T(8,128)(2,1)S(1)}, u32[]{:S(2)}, u32[]{:S(2)}) collective-permute-start(bf16[128,1024]{1,0:T(8,128)(2,1)S(1)} %get-tuple-element.67), channel_id=1, source_target_pairs={{0,96},{32,0},{64,32},{96,64},{1,97},{33,1},{65,33},{97,65},{2,98}... | collective-permute-start | bytes 786440 | tf_op jit(solution)/shard_map/ppermute | solution.py:363
  249.8 15.3 %collective-permute-start.23 = (bf16[128,1024]{1,0:T(8,128)(2,1)S(1)}, bf16[128,1024]{1,0:T(8,128)(2,1)S(1)}, u32[]{:S(2)}, u32[]{:S(2)}) collective-permute-start(bf16[128,1024]{1,0:T(8,128)(2,1)S(1)} %grad_pre.3.refs_0_), channel_id=1, source_target_pairs={{0,96},{32,0},{64,32},{96,64},{1,97},{33,1},{65,33},{97,65},{2,98}... | collective-permute-start | bytes 786440 | tf_op jit(solution)/shard_map/ppermute | solution.py:418
  252.5 22.8 %collective-permute-start.22 = (bf16[128,1024]{1,0:T(8,128)(2,1)S(1)}, bf16[128,1024]{1,0:T(8,128)(2,1)S(1)}, u32[]{:S(2)}, u32[]{:S(2)}) collective-permute-start(bf16[128,1024]{1,0:T(8,128)(2,1)S(1)} %grad_pre.3.refs_0_), channel_id=1, source_target_pairs={{0,64},{32,96},{64,0},{96,32},{1,65},{33,97},{65,1},{97,33},{2,66}... | collective-permute-start | bytes 786440 | tf_op jit(solution)/shard_map/ppermute | solution.py:418
  252.5 22.9 %collective-permute-start.21 = (bf16[128,1024]{1,0:T(8,128)(2,1)S(1)}, bf16[128,1024]{1,0:T(8,128)(2,1)S(1)}, u32[]{:S(2)}, u32[]{:S(2)}) collective-permute-start(bf16[128,1024]{1,0:T(8,128)(2,1)S(1)} %grad_pre.3.refs_0_), channel_id=1, source_target_pairs={{0,32},{32,64},{64,96},{96,0},{1,33},{33,65},{65,97},{97,1},{2,34}... | collective-permute-start | bytes 786440 | tf_op jit(solution)/shard_map/ppermute | solution.py:418
  (29 other events, 372.7 us)
